TPU v7x, 32 devices: a whole 2x2x4 slice. The times are simulated.
32 devices in a mesh: groups: 2 (over x), dp: 2 (over core), tensor: 8 (over z, y).
Axes of the slice: x: 2, y: 2, z: 4, core: 2. Of those that a mesh axis runs over, the one named last changes fastest.
Arguments:
- reward_hidden: bfloat16 [32, 256, 8192], P(('groups', 'dp'), None, 'tensor'), parts along dimension 0, may hold values from -6 to 6
- reward_gain: float32 [8192], P('tensor'), may hold values from 0.5 to 1.5
- reward_head: float32 [8192], P('tensor'), may hold values from -1 to 1
- decode_inputs: bfloat16 [2, 32, 8192], P(None, ('groups', 'dp'), 'tensor'), parts along dimension 1, may hold values from -6 to 6
- attn_gain: float32 [8192], replicated, may hold values from 0.5 to 1.5
- w_query: bfloat16 [8192, 8192], P(None, 'tensor'), may hold values from -0.0625 to 0.0625
- w_keyval: bfloat16 [8192, 2048], P(None, 'tensor'), may hold values from -0.0625 to 0.0625
- w_out: bfloat16 [8192, 8192], P('tensor'), may hold values from -3 to 3
- cache_keys: bfloat16 [32, 2048, 1024], P(('groups', 'dp'), 'tensor'), parts along dimension 0, may hold values from -720 to 720
- cache_values: bfloat16 [32, 2048, 1024], P(('groups', 'dp'), 'tensor'), parts along dimension 0, may hold values from -6 to 6
- lengths: int32 [32], P('groups'), parts along dimension 0, may hold values from 512 to 2048
- slot_map: int32 [32], P('groups'), parts along dimension 0, may hold values from 0 to 15, as said below
Outputs:
- reward: float32 [32], P(('groups', 'dp')), parts along dimension 0
- decoded: bfloat16 [2, 32, 8192], P(None, ('groups', 'dp'), 'tensor'), parts along dimension 1
There are 2 independent parts, one for each index of `groups`. A program takes and returns all parts, laid end to end along the dimension named above; an argument that names none is the same for every part. Nothing has to cross between parts.
Inputs may be any that keep to these rules, and one draw needn't show every extreme that they name: `slot_map`: each aligned block of 8 slots holds exactly 4 survivors, which map to themselves; every other slot maps to a survivor, and every survivor is named by exactly one other slot.
All inputs are finite; a program needn't handle non-finite values.
Results may differ from a plain program's by a relative error of at most 0.0055.
The roundings to bfloat16 on the way count: a program that leaves them out, or rounds other values in their place, can miss the bound.
Values may be sent and summed in bfloat16 or wider, within the bound.
No kernel may reach another device: no remote copies, remote signals or barrier semaphores. Data moves between devices by JAX's collectives and lax.ppermute only.
A program may use at most 128 MiB of HBM per device.

v0:
```python
import functools

import jax
import jax.numpy as jnp
from jax import lax
from jax.experimental import pallas as pl
from jax.experimental.pallas import tpu as pltpu
from jax.sharding import PartitionSpec as P


HD = 128
KVH = 8
STEPS = 2
PAIR = 2
LANES = 128
EXT = 8
EPS = 1e-05
NEG = -1e30
SCALE = HD ** (-0.5)
NT = (((1,), (1,)), ((), ()))
TN = (((0,), (0,)), ((), ()))
MIB = 1 << 20
ANY = pl.BlockSpec(memory_space=pl.ANY)
VMEM = pl.BlockSpec(memory_space=pltpu.VMEM)
SMEM = pl.BlockSpec(memory_space=pltpu.SMEM)


def iota(shape, dim):
    return lax.broadcasted_iota(jnp.int32, shape, dim)


def dot(a, b, dims=(((1,), (0,)), ((), ()))):
    return lax.dot_general(a, b, dims, preferred_element_type=jnp.float32)


def head_major(shape, pages, per_page, heads):
    o, s = iota(shape, 0), iota(shape, 1)
    row = o % per_page
    head = (o // per_page) % heads
    page = o // (per_page * heads)
    return (s == (head * pages + page) * per_page + row).astype(jnp.bfloat16)


def aligned(index, size):
    return pl.ds(pl.multiple_of(index * size, size), size)


def early_kernel(*refs):
    refs[-1][...] = jnp.zeros_like(refs[-1])


def plan_kernel(slots, steps, map_ref, length_ref, meta_ref, take_ref, give_ref, before_ref, place_ref):
    count = map_ref.shape[0]
    mine = lax.axis_index("dp")
    base = mine * slots
    for block in range(count // slots):
        found = jnp.int32(0)
        for s in range(block * slots, (block + 1) * slots):
            before_ref[s] = found
            found = found + (map_ref[s] == s).astype(jnp.int32)
    for s in range(slots):
        own = map_ref[base + s] == base + s

        @pl.when(own)
        def _():
            slot = before_ref[base + s]
            meta_ref[slot] = jnp.int32(s)
            meta_ref[slots // PAIR + slot] = length_ref[base + s]

    for r in range(count):
        source = map_ref[r]
        place_ref[r] = (
            lax.div(source, slots) * slots
            + PAIR * before_ref[source]
            + (source != r).astype(jnp.int32)
        )
    rows = slots * steps
    line, col = iota((rows, 2 * rows), 0), iota((rows, 2 * rows), 1)
    same = line % steps == (col // slots) % steps
    take = jnp.zeros((rows, 2 * rows), jnp.bool_)
    give = jnp.zeros((rows, 2 * rows), jnp.bool_)
    for side in range(2):
        start = base if side == 0 else (1 - mine) * slots
        for s in range(slots):
            target = place_ref[start + s] - base
            column = (col // rows == side) & (col % slots == s)
            take = take | (same & column & (line // steps == target))
    for s in range(slots):
        place = place_ref[base + s]
        far = (lax.div(place, slots) != mine).astype(jnp.int32)
        target = far * rows + lax.rem(place, slots) * steps
        give = give | ((line % slots == s) & (col == line // slots + target))
    take_ref[...] = take.astype(jnp.float32).astype(jnp.bfloat16)
    give_ref[...] = give.astype(jnp.float32).astype(jnp.bfloat16)


def reward_kernel(after_ref, hidden_ref, gain_ref, head_ref, *rest):
    out_ref, buffer, sems = rest[-3:]
    slots = hidden_ref.shape[0]
    loads = [
        pltpu.make_async_copy(hidden_ref.at[s], buffer.at[s], sems.at[s]) for s in range(slots)
    ]
    for load in loads:
        load.start()
    weight = gain_ref[...] * head_ref[...]
    for s in range(slots):
        loads[s].wait()
        hidden = buffer[s].astype(jnp.float32)
        for half, value in enumerate((hidden * hidden, hidden * weight)):
            sums = jnp.sum(value, axis=-1)
            if len(out_ref.shape) == 2:
                out_ref[half * slots + s] = sums
                continue
            for c in range(EXT // 4):
                piece = jnp.zeros((LANES,), jnp.float32)
                if c < sums.shape[0] // LANES:
                    piece = sums[c * LANES : (c + 1) * LANES]
                out_ref[s, half * (EXT // 4) + c] = piece


def choose_kernel(after_ref, take_ref, own_ref, far_ref, near_ref, both_ref, out_ref):
    for w, (a, b) in enumerate(((own_ref, far_ref), (near_ref, both_ref))):
        rows = jnp.concatenate([a[...], b[...]], axis=0)
        out_ref[w] = dot(take_ref[...], rows).astype(jnp.bfloat16)


def project_kernel(pages, per_page, width, x_ref, gain_ref, wq_ref, wkv_ref, out_ref):
    me = lax.axis_index("tensor")
    chunks, rows, depth = x_ref.shape
    total = jnp.zeros((rows, depth), jnp.float32)
    for r in range(chunks):
        part = x_ref[r].astype(jnp.float32)
        total = total + part * part
    inv = lax.rsqrt(jnp.sum(total, axis=-1, keepdims=True) / width + EPS)

    query = jnp.zeros((rows, wq_ref.shape[1]), jnp.float32)
    keyval = jnp.zeros((rows, wkv_ref.shape[1]), jnp.float32)
    for r in range(chunks):
        normed = (x_ref[r].astype(jnp.float32) * inv * gain_ref[me ^ r]).astype(jnp.bfloat16)
        query = query + dot(normed, wq_ref[aligned(me ^ r, depth), :])
        keyval = keyval + dot(normed, wkv_ref[aligned(me ^ r, depth), :])

    heads = query.shape[1] // HD
    query = query.astype(jnp.bfloat16)
    stacked = jnp.concatenate([query[:, h * HD : (h + 1) * HD] for h in range(heads)], axis=0)
    order = head_major((rows * heads, rows * heads), pages, per_page, heads)
    body = rows * heads
    out_ref[:body] = dot(order, stacked).astype(jnp.bfloat16)
    keyval = keyval.astype(jnp.bfloat16)
    columns = keyval.shape[1]
    if columns < LANES:
        pad = jnp.zeros((rows, LANES - columns), jnp.bfloat16)
        keyval = jnp.concatenate([keyval, pad], axis=1)
    for v in range(keyval.shape[1] // LANES):
        out_ref[body + v * rows : body + (v + 1) * rows] = keyval[:, v * LANES : (v + 1) * LANES]


def attend_kernel(pages, page_rows, meta_ref, q_ref, k_ref, v_ref, reward_ref, *rest):
    outs, (spread, product) = rest[:-2], rest[-2:]
    width = k_ref.shape[1]
    span = KVH * page_rows
    body = pages * page_rows
    first = lax.axis_index("tensor") * width
    me = lax.axis_index("tensor") if len(outs) > 1 else 0
    spread[...] = jnp.zeros_like(spread)
    share = LANES // page_rows
    tops, totals = [], []
    for i in range(pages):
        for r in range(KVH):
            spread[i, r * page_rows : (r + 1) * page_rows, aligned(me ^ r, HD)] = q_ref[
                r, i * page_rows : (i + 1) * page_rows, :
            ]
        scores = dot(k_ref[meta_ref[i]], spread[i], NT) * SCALE
        valid = first + iota((width, span), 0) < meta_ref[pages + i]
        scores = jnp.where(valid, scores, NEG)
        top = jnp.max(scores, axis=0, keepdims=True)
        expo = jnp.where(valid, jnp.exp(scores - top), 0.0)
        total = jnp.sum(expo, axis=0, keepdims=True)
        weights = expo.astype(jnp.bfloat16)
        for part in range(KVH // share):
            values = v_ref[meta_ref[i], :, aligned(part ^ lax.div(me, share), share * HD)]
            lines = slice(part * share * page_rows, (part + 1) * share * page_rows)
            product[i, lines] = dot(weights[:, lines], values, TN)
        for r in range(KVH):
            out = outs[r] if len(outs) > 1 else outs[0].at[r]
            out[i * page_rows : (i + 1) * page_rows, :] = product[
                i, r * page_rows : (r + 1) * page_rows, aligned((me ^ r) & (share - 1), HD)
            ]
        tops.append(top)
        totals.append(total)
    held = iota((1, LANES), 1) // page_rows
    stats = []
    for part in range(KVH // share):
        lanes = slice(part * LANES, (part + 1) * LANES)
        tile = jnp.concatenate([x[:, lanes] for x in tops + totals], axis=0)
        turned = [tile] + [pltpu.roll(tile, t * page_rows, 1) for t in range(1, share)]
        for q in range(share):
            for skip in (0, pages):
                line = jnp.zeros((1, LANES), jnp.float32)
                for i in range(pages):
                    row = turned[(i - q) % share][skip + i : skip + i + 1]
                    line = jnp.where(held == i, row, line)
                stats.append(line)
    for r in range(KVH):
        out = outs[r] if len(outs) > 1 else outs[0].at[r]
        out[body : body + 2, :] = jnp.concatenate(stats[2 * r : 2 * r + 2], axis=0)
        if len(outs) > 1:
            out[body + 2 : body + 4, :] = jnp.zeros((2, LANES), jnp.float32)
            out[body + 4 :, :] = reward_ref[me ^ r]
        else:
            out[body + 2 :, :] = jnp.zeros((EXT - 2, LANES), jnp.float32)


def merge_kernel(pages, per_page, width, span, slots, chunks, q_ref, gathered_ref, w_ref, *rest):
    att = rest[-1]
    split = len(rest) > 3
    parts = rest[:chunks] if split else [rest[0].at[b] for b in range(chunks)]
    outs = rest[chunks:-1] if split else rest[1:-1]
    me = lax.axis_index("tensor")
    body = parts[0].shape[0] - EXT
    page_rows = body // pages
    heads = page_rows // per_page
    rows = pages * per_page

    kv_head = lax.div(me * heads, heads * chunks // KVH)
    if split:
        pieces = (gathered_ref.shape[1] - body) // rows

        def fresh_of(column):
            source = lax.div(column, pieces) ^ me
            start = pl.multiple_of(body + lax.rem(column, pieces) * rows, rows)
            return gathered_ref[source, pl.ds(start, rows), :]

        fresh_k, fresh_v = fresh_of(kv_head), fresh_of(KVH + kv_head)
    else:
        fresh_k, fresh_v = gathered_ref[kv_head], gathered_ref[KVH + kv_head]

    query = q_ref[:body, :]
    recent = dot(query, fresh_k, NT) * SCALE
    line, col = iota(recent.shape, 0), iota(recent.shape, 1)
    mine = (line // page_rows) * per_page + line % per_page
    seen = (mine // STEPS == col // STEPS) & (col <= mine)
    recent = jnp.where(seen, recent, NEG)
    recent_max = jnp.max(recent, axis=-1, keepdims=True)
    recent_exp = jnp.where(seen, jnp.exp(recent - recent_max), 0.0)
    recent_total = jnp.sum(recent_exp, axis=-1, keepdims=True)
    recent_acc = dot(recent_exp.astype(jnp.bfloat16), fresh_v)

    maxima = [parts[b][body : body + 1, :] for b in range(chunks)]
    totals = [parts[b][body + 1 : body + 2, :] for b in range(chunks)]
    top = functools.reduce(jnp.maximum, maxima)
    factors = [jnp.exp(m - top) for m in maxima]
    total = functools.reduce(jnp.add, [f * t for f, t in zip(factors, totals)])

    pick = iota((body, LANES), 0) == iota((body, LANES), 1)

    def column(packed):
        wide = jnp.where(pick, jnp.broadcast_to(packed, pick.shape), 0.0)
        return jnp.sum(wide, axis=-1, keepdims=True)

    acc = jnp.zeros((body, HD), jnp.float32)
    for b in range(chunks):
        acc = acc + column(factors[b]) * parts[b][:body, :]
    cache_top, cache_total = column(top), column(total)
    top = jnp.maximum(cache_top, recent_max)
    cache_factor = jnp.exp(cache_top - top)
    recent_factor = jnp.exp(recent_max - top)
    total = cache_factor * cache_total + recent_factor * recent_total
    acc = cache_factor * acc + recent_factor * recent_acc
    attended = (acc / total).astype(jnp.bfloat16)
    order = head_major((body, body), pages, per_page, heads)
    attended = dot(order, attended, TN).astype(jnp.bfloat16)
    for h in range(heads):
        att[:, h * HD : (h + 1) * HD] = attended[h * rows : (h + 1) * rows]

    tile = functools.reduce(jnp.add, [parts[b][body + EXT // 2 :, :] for b in range(chunks)])
    used = EXT // 4
    value = tile[used:] * lax.rsqrt(tile[:used] / width + EPS)
    mean = jnp.sum(value, keepdims=True) / span
    own = lax.div(me * (slots * span // chunks), span)
    mean = jnp.where(iota((EXT, LANES), 0) == own, mean, 0.0)

    part = w_ref.shape[1] // chunks
    for r in range(chunks):
        out = outs[r] if split else outs[0].at[me ^ r]
        product = dot(att[...], w_ref[:, aligned(me ^ r, part)])
        for c in range(part // LANES):
            out[c * rows : (c + 1) * rows, :] = product[:, c * LANES : (c + 1) * LANES]
        out[out.shape[0] - EXT :, :] = mean


def sum_kernel(rows, *refs):
    parts, (out_ref, reward_ref) = refs[:-2], refs[-2:]
    if len(parts) == 1:
        parts = [parts[0].at[b] for b in range(parts[0].shape[0])]
    total = parts[0][...]
    for part in parts[1:]:
        total = total + part[...]
    for c in range(out_ref.shape[1] // LANES):
        out_ref[:, c * LANES : (c + 1) * LANES] = total[c * rows : (c + 1) * rows].astype(
            jnp.bfloat16
        )
    reward_ref[...] = total[total.shape[0] - EXT :]


LINE = (6, 2, 4)
ALL = (6, 1, 7, 2, 5, 3, 4)


def partner(x, chunks, bits):
    return lax.ppermute(x, "tensor", [(i, i ^ bits) for i in range(chunks)])


def spread_line(pair, chunks):
    others = {bits: partner(pair, chunks, bits) for bits in LINE}
    stacked = jnp.stack([pair] + [others[bits] for bits in sorted(LINE)])
    return stacked.reshape((chunks,) + pair.shape[1:])


def spread_all(x, chunks, index):
    if chunks != KVH:
        every = jnp.broadcast_to(x[None], (chunks,) + x.shape)
        every = lax.all_to_all(every, "tensor", 0, 0, tiled=True)
        return jnp.take(every, index ^ jnp.arange(chunks), axis=0), x
    pair = jnp.stack([x, partner(x, chunks, 1)])
    return spread_line(pair, chunks), pair


def trade(blocks, chunks):
    if len(blocks) == 1:
        return [lax.all_to_all(blocks[0], "tensor", 0, 0, tiled=True)]
    traded = {bits: partner(blocks[bits], chunks, bits) for bits in ALL}
    return [blocks[0]] + [traded[bits] for bits in range(1, chunks)]


def local(
    chunks,
    reward_hidden,
    reward_gain,
    reward_head,
    decode_inputs,
    attn_gain,
    w_query,
    w_keyval,
    w_out,
    cache_keys,
    cache_values,
    lengths,
    slot_map,
):
    slots, width = cache_keys.shape[:2]
    depth, qcols = w_query.shape
    kvcols = w_keyval.shape[1]
    part = decode_inputs.shape[-1]
    heads = qcols // HD
    group = heads * chunks // KVH
    split = group // heads
    pages = slots // PAIR
    per_page = PAIR * STEPS
    page_rows = per_page * group
    rows = slots * STEPS
    body = rows * heads
    index = lax.axis_index("tensor")
    swap = [(0, 1), (1, 0)]
    direct = chunks == KVH

    meta, take, give = pl.pallas_call(
        functools.partial(plan_kernel, slots, STEPS),
        in_specs=[SMEM, SMEM],
        out_specs=[SMEM, VMEM, VMEM],
        out_shape=(
            jax.ShapeDtypeStruct((2 * pages,), jnp.int32),
            jax.ShapeDtypeStruct((rows, 2 * rows), jnp.bfloat16),
            jax.ShapeDtypeStruct((rows, 2 * rows), jnp.bfloat16),
        ),
        scratch_shapes=[
            pltpu.SMEM(slot_map.shape, jnp.int32),
            pltpu.SMEM(slot_map.shape, jnp.int32),
        ],
        compiler_params=pltpu.CompilerParams(vmem_limit_bytes=MIB),
        name="plan",
    )(slot_map, lengths)

    early = pl.pallas_call(
        early_kernel,
        in_specs=[ANY] * 3,
        out_specs=VMEM,
        out_shape=jax.ShapeDtypeStruct((EXT, LANES), jnp.float32),
        compiler_params=pltpu.CompilerParams(vmem_limit_bytes=38 * MIB),
        name="early",
    )(w_out, w_out, w_out)
    own = decode_inputs.reshape(rows, part)
    far = lax.ppermute(own, "dp", swap)
    if direct:
        near = partner(own, chunks, 1)
        cross = [
            (d * chunks + t, (1 - d) * chunks + (t ^ 1)) for d in range(2) for t in range(chunks)
        ]
        both = lax.ppermute(own, ("dp", "tensor"), cross)
        pair = pl.pallas_call(
            choose_kernel,
            in_specs=[ANY] + [VMEM] * 5,
            out_specs=VMEM,
            out_shape=jax.ShapeDtypeStruct((2, rows, part), jnp.bfloat16),
            compiler_params=pltpu.CompilerParams(vmem_limit_bytes=MIB),
            name="choose",
        )(early, take, own, far, near, both)
        tokens = spread_line(pair, chunks)
    else:
        chosen = dot(take, jnp.concatenate([own, far], axis=0)).astype(jnp.bfloat16)
        tokens, _ = spread_all(chosen, chunks, index)

    pieces = max(kvcols // LANES, 1)
    packed_rows = body + pieces * rows
    packed = pl.pallas_call(
        functools.partial(project_kernel, pages, per_page, depth),
        in_specs=[VMEM] * 4,
        out_specs=VMEM,
        out_shape=jax.ShapeDtypeStruct((packed_rows, LANES), jnp.bfloat16),
        compiler_params=pltpu.CompilerParams(vmem_limit_bytes=4 * MIB),
        cost_estimate=pl.CostEstimate(
            flops=2 * rows * depth * (qcols + kvcols),
            bytes_accessed=2 * depth * (qcols + kvcols),
            transcendentals=0,
        ),
        name="project",
    )(tokens, attn_gain.reshape(chunks, 1, part), w_query, w_keyval)
    gathered, after = spread_all(packed, chunks, index)

    span = reward_hidden.shape[1]
    tiled = direct and slots == chunks and span <= EXT // 4 * LANES
    reward_parts = pl.pallas_call(
        reward_kernel,
        in_specs=[ANY, ANY, VMEM, VMEM] + [ANY] * 0,
        out_specs=VMEM,
        out_shape=jax.ShapeDtypeStruct(
            (slots, EXT // 2, LANES) if tiled else (2 * slots, span), jnp.float32
        ),
        scratch_shapes=[
            pltpu.VMEM(reward_hidden.shape, reward_hidden.dtype),
            pltpu.SemaphoreType.DMA((slots,)),
        ],
        compiler_params=pltpu.CompilerParams(vmem_limit_bytes=8 * MIB),
        cost_estimate=pl.CostEstimate(
            flops=4 * reward_hidden.size,
            bytes_accessed=2 * reward_hidden.size,
            transcendentals=0,
        ),
        name="reward",
    )(after, reward_hidden, reward_gain[None], reward_head[None])

    def tile(values):
        values = values.reshape(chunks, -1)
        size = EXT // 4 * LANES
        return jnp.pad(values, ((0, 0), (0, size - values.shape[1]))).reshape(
            chunks, EXT // 4, LANES
        )

    if not tiled:
        reward_parts = jnp.concatenate(
            [tile(reward_parts[:slots]), tile(reward_parts[slots:])], axis=1
        )
    fresh = gathered
    if not direct:
        fresh = jnp.take(gathered[:, body:, :kvcols], index ^ jnp.arange(chunks), axis=0)
        fresh = fresh.transpose(1, 0, 2).reshape(rows, 2 * KVH, HD).transpose(1, 0, 2)
    queries = gathered
    if not direct:
        queries = (
            jnp.take(gathered[:, :body], index ^ jnp.arange(chunks), axis=0)
            .reshape(KVH, split, pages, heads * per_page, HD)
            .transpose(0, 2, 1, 3, 4)
            .reshape(KVH, pages * page_rows, HD)
        )

    big = pages * page_rows
    block = (big + EXT, HD)
    attended = pl.pallas_call(
        functools.partial(attend_kernel, pages, page_rows),
        in_specs=[SMEM] + [VMEM] * 4,
        out_specs=[VMEM] * (KVH if direct else 1),
        out_shape=(
            [jax.ShapeDtypeStruct(block, jnp.float32)] * KVH
            if direct
            else [jax.ShapeDtypeStruct((KVH,) + block, jnp.float32)]
        ),
        scratch_shapes=[
            pltpu.VMEM((pages, KVH * page_rows, KVH * HD), jnp.bfloat16),
            pltpu.VMEM((pages, KVH * page_rows, LANES // page_rows * HD), jnp.float32),
        ],
        compiler_params=pltpu.CompilerParams(vmem_limit_bytes=10 * MIB),
        cost_estimate=pl.CostEstimate(
            flops=4 * pages * width * KVH * HD * KVH * page_rows,
            bytes_accessed=4 * pages * width * KVH * HD,
            transcendentals=pages * width * KVH * page_rows,
        ),
        name="attend",
    )(meta, queries, cache_keys, cache_values, reward_parts)
    if not direct:
        acc = (
            attended[0][:, :big]
            .reshape(KVH, pages, split, heads * per_page, HD)
            .transpose(0, 2, 1, 3, 4)
            .reshape(chunks, body, HD)
        )
        extra = attended[0][:, big : big + 2].reshape(KVH, 2, pages, split, heads * per_page)
        extra = extra.transpose(0, 3, 1, 2, 4).reshape(chunks, 2, body)
        extra = jnp.pad(extra, ((0, 0), (0, 2), (0, LANES - body)))
        attended = [jnp.concatenate([acc, extra, reward_parts], axis=1)]
    parts = trade(attended, chunks)

    chunk_rows = part // LANES * rows + EXT
    partial = pl.pallas_call(
        functools.partial(merge_kernel, pages, per_page, depth, span, slots, chunks),
        in_specs=[VMEM] * (3 + len(parts)),
        out_specs=[VMEM] * len(parts),
        out_shape=(
            [jax.ShapeDtypeStruct((chunk_rows, LANES), jnp.float32)] * chunks
            if direct
            else [jax.ShapeDtypeStruct((chunks, chunk_rows, LANES), jnp.float32)]
        ),
        scratch_shapes=[pltpu.VMEM((rows, qcols), jnp.bfloat16)],
        compiler_params=pltpu.CompilerParams(vmem_limit_bytes=8 * MIB),
        cost_estimate=pl.CostEstimate(
            flops=2 * rows * qcols * depth, bytes_accessed=2 * qcols * depth, transcendentals=0
        ),
        name="merge",
    )(packed, fresh, w_out, *parts)
    partial = trade(partial, chunks)

    decoded, reward = pl.pallas_call(
        functools.partial(sum_kernel, rows),
        out_shape=(
            jax.ShapeDtypeStruct((rows, part), jnp.bfloat16),
            jax.ShapeDtypeStruct((EXT, LANES), jnp.float32),
        ),
        compiler_params=pltpu.CompilerParams(vmem_limit_bytes=8 * MIB),
        name="total",
    )(*partial)
    far = lax.ppermute(decoded, "dp", swap)
    decoded = dot(give, jnp.concatenate([decoded, far], axis=0)).astype(jnp.bfloat16)
    return (reward[:slots, 0], decoded.reshape(STEPS, slots, part))


def solution(mesh):
    chunks = mesh.shape["tensor"]

    def body(*arrays):
        return local(chunks, *arrays)

    return jax.shard_map(
        body,
        mesh=mesh,
        in_specs=(
            P(("groups", "dp"), None, "tensor"),
            P("tensor"),
            P("tensor"),
            P(None, ("groups", "dp"), "tensor"),
            P(),
            P(None, "tensor"),
            P(None, "tensor"),
            P("tensor", None),
            P(("groups", "dp"), "tensor", None),
            P(("groups", "dp"), "tensor", None),
            P("groups"),
            P("groups"),
        ),
        out_specs=(P(("groups", "dp")), P(None, ("groups", "dp"), "tensor")),
        check_vma=False,
    )
```

profile of v0, /device:TPU:0, one launch (start us, length us, event | category | flops | bytes accessed | tf_op | source)
XLA Modules:
  0.0 73.8 jit_solution(6474276622421963469)
XLA Ops:
  0.7 2.5 %collective-permute-start.2 = (bf16[16,1024]{1,0:T(8,128)(2,1)}, bf16[16,1024]{1,0:T(8,128)(2,1)S(1)}, u32[]{:S(2)}, u32[]{:S(2)}) collective-permute-start(bf16[16,1024]{1,0:T(8,128)(2,1)} %bitcast.30), channel_id=1, source_target_pairs={{0,9},{1,8},{2,11},{3,10},{4,13},{5,12},{6,15},{7,14},{8,1},{9,0},... | collective-permute-start | bytes 98312 | tf_op jit(solution)/shard_map/ppermute | solution.py:399
  5.3 2.1 %collective-permute-done.1.near_ref = bf16[16,1024]{1,0:T(8,128)(2,1)S(1)} collective-permute-done((bf16[16,1024]{1,0:T(8,128)(2,1)}, bf16[16,1024]{1,0:T(8,128)(2,1)S(1)}, u32[]{:S(2)}, u32[]{:S(2)}) %collective-permute-start.1) | collective-permute-done | bytes 32800 | tf_op jit(solution)/shard_map/ppermute | solution.py:311
  7.6 3.7 %collective-permute-start.5 = (bf16[2,16,1024]{2,1,0:T(8,128)(2,1)S(1)}, bf16[2,16,1024]{2,1,0:T(8,128)(2,1)S(1)}, u32[]{:S(2)}, u32[]{:S(2)}) collective-permute-start(bf16[2,16,1024]{2,1,0:T(8,128)(2,1)S(1)} %choose.1), channel_id=1, source_target_pairs={{0,6},{1,7},{2,4},{3,5},{4,2},{5,3},{6,0},{7,1},{8,14},{9,15},{10,... | collective-permute-start | bytes 196616 | tf_op jit(solution)/shard_map/ppermute | solution.py:311
  12.0 2.1 %collective-permute-done.5 = bf16[2,16,1024]{2,1,0:T(8,128)(2,1)S(1)} collective-permute-done((bf16[2,16,1024]{2,1,0:T(8,128)(2,1)S(1)}, bf16[2,16,1024]{2,1,0:T(8,128)(2,1)S(1)}, u32[]{:S(2)}, u32[]{:S(2)}) %collective-permute-start.5) | collective-permute-done | bytes 65568 | tf_op jit(solution)/shard_map/ppermute | solution.py:311
  14.1 2.7 %collective-permute-done.4 = bf16[2,16,1024]{2,1,0:T(8,128)(2,1)S(1)} collective-permute-done((bf16[2,16,1024]{2,1,0:T(8,128)(2,1)S(1)}, bf16[2,16,1024]{2,1,0:T(8,128)(2,1)S(1)}, u32[]{:S(2)}, u32[]{:S(2)}) %collective-permute-start.4) | collective-permute-done | bytes 65568 | tf_op jit(solution)/shard_map/ppermute | solution.py:311
  17.0 3.1 %project.1.q_ref = bf16[160,128]{1,0:T(8,128)(2,1)S(1)} custom-call(bf16[8,16,1024]{2,1,0:T(8,128)(2,1)S(1)} %bitcast.26, f32[8,1,1024]{2,1,0:T(1,128)S(1)} %bitcast.29, bf16[8192,1024]{1,0:T(8,128)(2,1)S(1)} %bitcast.23, bf16[8192,256]{1,0:T(8,128)(2,1)S(1)} %copy-done), custom_call_target="tpu_custom_call" | custom-call | flops 335544320 | bytes 20971520 | tf_op jit(solution)/shard_map/project/pallas_call | solution.py:415
  21.5 2.7 %collective-permute-done.6 = bf16[160,128]{1,0:T(8,128)(2,1)S(1)} collective-permute-done((bf16[160,128]{1,0:T(8,128)(2,1)S(1)}, bf16[160,128]{1,0:T(8,128)(2,1)S(1)}, u32[]{:S(2)}, u32[]{:S(2)}) %collective-permute-start.6) | collective-permute-done | bytes 40992 | tf_op jit(solution)/shard_map/ppermute | solution.py:311
  24.2 2.8 %collective-permute-start.9 = (bf16[2,160,128]{2,1,0:T(8,128)(2,1)S(1)}, bf16[2,160,128]{2,1,0:T(8,128)(2,1)S(1)}, u32[]{:S(2)}, u32[]{:S(2)}) collective-permute-start(bf16[2,160,128]{2,1,0:T(8,128)(2,1)S(1)} %get-tuple-element.45.after_ref), channel_id=1, source_target_pairs={{0,6},{1,7},{2,4},{3,5},{4,2},{5,3},{6,0},{7,1},{8,14},{9,15},{10,... | collective-permute-start | bytes 245768 | tf_op jit(solution)/shard_map/ppermute | solution.py:311
  28.7 2.3 %reward.1.reward_ref = f32[8,4,128]{2,1,0:T(4,128)S(1)} custom-call(bf16[2,160,128]{2,1,0:T(8,128)(2,1)S(1)} %get-tuple-element.45.after_ref, bf16[8,256,1024]{2,1,0:T(8,128)(2,1)S(1)} %copy-done.1, f32[1,1024]{1,0:T(1,128)S(1)} %bitcast.34, f32[1,1024]{1,0:T(1,128)S(1)} %bitcast.35), custom_call_target="tpu_custom_call" | custom-call | flops 8388608 | bytes 4194304 | tf_op jit(solution)/shard_map/reward/pallas_call | solution.py:432
  31.0 2.5 %collective-permute-done.8 = bf16[2,160,128]{2,1,0:T(8,128)(2,1)S(1)} collective-permute-done((bf16[2,160,128]{2,1,0:T(8,128)(2,1)S(1)}, bf16[2,160,128]{2,1,0:T(8,128)(2,1)S(1)}, u32[]{:S(2)}, u32[]{:S(2)}) %collective-permute-start.8) | collective-permute-done | bytes 81952 | tf_op jit(solution)/shard_map/ppermute | solution.py:311
  33.5 3.2 %attend.1 = (f32[136,128]{1,0:T(8,128)S(1)}, f32[136,128]{1,0:T(8,128)S(1)}, f32[136,128]{1,0:T(8,128)S(1)}, f32[136,128]{1,0:T(8,128)S(1)}, f32[136,128]{1,0:T(...) custom-call(s32[8]{0:T(128)S(1)} %get-tuple-element.24.meta_ref, ...), custom_call_target="tpu_custom_call" | custom-call | flops 1073741824 | bytes 4194304 | tf_op jit(solution)/shard_map/attend/pallas_call | solution.py:478
  38.0 2.4 %collective-permute-start.12 = (f32[136,128]{1,0:T(8,128)S(1)}, f32[136,128]{1,0:T(8,128)S(1)}, u32[]{:S(2)}, u32[]{:S(2)}) collective-permute-start(f32[136,128]{1,0:T(8,128)S(1)} %get-tuple-element.28), channel_id=1, source_target_pairs={{0,3},{1,2},{2,1},{3,0},{4,7},{5,6},{6,5},{7,4},{8,11},{9,10},{10,... | collective-permute-start | bytes 208904 | tf_op jit(solution)/shard_map/ppermute | solution.py:311
  41.2 2.6 %collective-permute-start.14 = (f32[136,128]{1,0:T(8,128)S(1)}, f32[136,128]{1,0:T(8,128)S(1)}, u32[]{:S(2)}, u32[]{:S(2)}) collective-permute-start(f32[136,128]{1,0:T(8,128)S(1)} %get-tuple-element.30), channel_id=1, source_target_pairs={{0,5},{1,4},{2,7},{3,6},{4,1},{5,0},{6,3},{7,2},{8,13},{9,12},{10,... | collective-permute-start | bytes 208904 | tf_op jit(solution)/shard_map/ppermute | solution.py:311
  43.8 2.1 %collective-permute-start.15 = (f32[136,128]{1,0:T(8,128)S(1)}, f32[136,128]{1,0:T(8,128)S(1)}, u32[]{:S(2)}, u32[]{:S(2)}) collective-permute-start(f32[136,128]{1,0:T(8,128)S(1)} %get-tuple-element.31), channel_id=1, source_target_pairs={{0,6},{1,7},{2,4},{3,5},{4,2},{5,3},{6,0},{7,1},{8,14},{9,15},{10,... | collective-permute-start | bytes 208904 | tf_op jit(solution)/shard_map/ppermute | solution.py:311
  45.9 2.0 %collective-permute-start.16 = (f32[136,128]{1,0:T(8,128)S(1)}, f32[136,128]{1,0:T(8,128)S(1)}, u32[]{:S(2)}, u32[]{:S(2)}) collective-permute-start(f32[136,128]{1,0:T(8,128)S(1)} %get-tuple-element.32), channel_id=1, source_target_pairs={{0,7},{1,6},{2,5},{3,4},{4,3},{5,2},{6,1},{7,0},{8,15},{9,14},{10,... | collective-permute-start | bytes 208904 | tf_op jit(solution)/shard_map/ppermute | solution.py:311
  48.0 2.3 %collective-permute-done.13.rest_4_ = f32[136,128]{1,0:T(8,128)S(1)} collective-permute-done((f32[136,128]{1,0:T(8,128)S(1)}, f32[136,128]{1,0:T(8,128)S(1)}, u32[]{:S(2)}, u32[]{:S(2)}) %collective-permute-start.13) | collective-permute-done | bytes 69664 | tf_op jit(solution)/shard_map/ppermute | solution.py:311
  50.3 1.8 %collective-permute-done.14.rest_5_ = f32[136,128]{1,0:T(8,128)S(1)} collective-permute-done((f32[136,128]{1,0:T(8,128)S(1)}, f32[136,128]{1,0:T(8,128)S(1)}, u32[]{:S(2)}, u32[]{:S(2)}) %collective-permute-start.14) | collective-permute-done | bytes 69664 | tf_op jit(solution)/shard_map/ppermute | solution.py:311
  53.1 2.8 %merge.1 = (f32[136,128]{1,0:T(8,128)S(1)}, f32[136,128]{1,0:T(8,128)S(1)}, f32[136,128]{1,0:T(8,128)S(1)}, f32[136,128]{1,0:T(8,128)S(1)}, f32[136,128]{1,0:T(8...) custom-call(bf16[160,128]{1,0:T(8,128)(2,1)S(1)} %project.1.q_ref, ...), custom_call_target="tpu_custom_call" | custom-call | flops 268435456 | bytes 16777216 | tf_op jit(solution)/shard_map/merge/pallas_call | solution.py:513
  56.4 2.0 %collective-permute-start.18 = (f32[136,128]{1,0:T(8,128)S(1)}, f32[136,128]{1,0:T(8,128)S(1)}, u32[]{:S(2)}, u32[]{:S(2)}) collective-permute-start(f32[136,128]{1,0:T(8,128)S(1)} %get-tuple-element.35), channel_id=1, source_target_pairs={{0,2},{1,3},{2,0},{3,1},{4,6},{5,7},{6,4},{7,5},{8,10},{9,11},{10,... | collective-permute-start | bytes 208904 | tf_op jit(solution)/shard_map/ppermute | solution.py:311
  59.4 2.6 %collective-permute-start.20 = (f32[136,128]{1,0:T(8,128)S(1)}, f32[136,128]{1,0:T(8,128)S(1)}, u32[]{:S(2)}, u32[]{:S(2)}) collective-permute-start(f32[136,128]{1,0:T(8,128)S(1)} %get-tuple-element.37), channel_id=1, source_target_pairs={{0,4},{1,5},{2,6},{3,7},{4,0},{5,1},{6,2},{7,3},{8,12},{9,13},{10,... | collective-permute-start | bytes 208904 | tf_op jit(solution)/shard_map/ppermute | solution.py:311
  62.3 2.1 %collective-permute-start.22 = (f32[136,128]{1,0:T(8,128)S(1)}, f32[136,128]{1,0:T(8,128)S(1)}, u32[]{:S(2)}, u32[]{:S(2)}) collective-permute-start(f32[136,128]{1,0:T(8,128)S(1)} %get-tuple-element.39), channel_id=1, source_target_pairs={{0,6},{1,7},{2,4},{3,5},{4,2},{5,3},{6,0},{7,1},{8,14},{9,15},{10,... | collective-permute-start | bytes 208904 | tf_op jit(solution)/shard_map/ppermute | solution.py:311
  64.4 2.6 %collective-permute-start.23 = (f32[136,128]{1,0:T(8,128)S(1)}, f32[136,128]{1,0:T(8,128)S(1)}, u32[]{:S(2)}, u32[]{:S(2)}) collective-permute-start(f32[136,128]{1,0:T(8,128)S(1)} %get-tuple-element.40), channel_id=1, source_target_pairs={{0,7},{1,6},{2,5},{3,4},{4,3},{5,2},{6,1},{7,0},{8,15},{9,14},{10,... | collective-permute-start | bytes 208904 | tf_op jit(solution)/shard_map/ppermute | solution.py:311
  67.0 2.0 %collective-permute-done.20.refs_4_ = f32[136,128]{1,0:T(8,128)S(1)} collective-permute-done((f32[136,128]{1,0:T(8,128)S(1)}, f32[136,128]{1,0:T(8,128)S(1)}, u32[]{:S(2)}, u32[]{:S(2)}) %collective-permute-start.20) | collective-permute-done | bytes 69664 | tf_op jit(solution)/shard_map/ppermute | solution.py:311
  69.0 2.7 %collective-permute-done.21.refs_5_ = f32[136,128]{1,0:T(8,128)S(1)} collective-permute-done((f32[136,128]{1,0:T(8,128)S(1)}, f32[136,128]{1,0:T(8,128)S(1)}, u32[]{:S(2)}, u32[]{:S(2)}) %collective-permute-start.21) | collective-permute-done | bytes 69664 | tf_op jit(solution)/shard_map/ppermute | solution.py:311
  (77 shorter events, 13.2 us)
Async XLA Ops:
  0.7 4.6 %collective-permute-start.2 = (bf16[16,1024]{1,0:T(8,128)(2,1)}, bf16[16,1024]{1,0:T(8,128)(2,1)S(1)}, u32[]{:S(2)}, u32[]{:S(2)}) collective-permute-start(bf16[16,1024]{1,0:T(8,128)(2,1)} %bitcast.30), channel_id=1, source_target_pairs={{0,9},{1,8},{2,11},{3,10},{4,13},{5,12},{6,15},{7,14},{8,1},{9,0},... | collective-permute-start | bytes 98312 | tf_op jit(solution)/shard_map/ppermute | solution.py:399
  3.2 4.2 %collective-permute-start.1 = (bf16[16,1024]{1,0:T(8,128)(2,1)}, bf16[16,1024]{1,0:T(8,128)(2,1)S(1)}, u32[]{:S(2)}, u32[]{:S(2)}) collective-permute-start(bf16[16,1024]{1,0:T(8,128)(2,1)} %bitcast.31), channel_id=1, source_target_pairs={{0,1},{1,0},{2,3},{3,2},{4,5},{5,4},{6,7},{7,6},{8,9},{9,8},{10,11... | collective-permute-start | bytes 98312 | tf_op jit(solution)/shard_map/ppermute | solution.py:311
  3.9 3.5 %collective-permute-start = (bf16[16,1024]{1,0:T(8,128)(2,1)}, bf16[16,1024]{1,0:T(8,128)(2,1)S(1)}, u32[]{:S(2)}, u32[]{:S(2)}) collective-permute-start(bf16[16,1024]{1,0:T(8,128)(2,1)} %bitcast.32), channel_id=1, source_target_pairs={{0,8},{8,0},{1,9},{9,1},{2,10},{10,2},{3,11},{11,3},{4,12},{12,4},... | collective-permute-start | bytes 98312 | tf_op jit(solution)/shard_map/ppermute | solution.py:393
  7.6 6.6 %collective-permute-start.5 = (bf16[2,16,1024]{2,1,0:T(8,128)(2,1)S(1)}, bf16[2,16,1024]{2,1,0:T(8,128)(2,1)S(1)}, u32[]{:S(2)}, u32[]{:S(2)}) collective-permute-start(bf16[2,16,1024]{2,1,0:T(8,128)(2,1)S(1)} %choose.1), channel_id=1, source_target_pairs={{0,6},{1,7},{2,4},{3,5},{4,2},{5,3},{6,0},{7,1},{8,14},{9,15},{10,... | collective-permute-start | bytes 196616 | tf_op jit(solution)/shard_map/ppermute | solution.py:311
  11.2 5.6 %collective-permute-start.4 = (bf16[2,16,1024]{2,1,0:T(8,128)(2,1)S(1)}, bf16[2,16,1024]{2,1,0:T(8,128)(2,1)S(1)}, u32[]{:S(2)}, u32[]{:S(2)}) collective-permute-start(bf16[2,16,1024]{2,1,0:T(8,128)(2,1)S(1)} %choose.1), channel_id=1, source_target_pairs={{0,4},{1,5},{2,6},{3,7},{4,0},{5,1},{6,2},{7,3},{8,12},{9,13},{10,... | collective-permute-start | bytes 196616 | tf_op jit(solution)/shard_map/ppermute | solution.py:311
  11.2 5.6 %collective-permute-start.3 = (bf16[2,16,1024]{2,1,0:T(8,128)(2,1)S(1)}, bf16[2,16,1024]{2,1,0:T(8,128)(2,1)S(1)}, u32[]{:S(2)}, u32[]{:S(2)}) collective-permute-start(bf16[2,16,1024]{2,1,0:T(8,128)(2,1)S(1)} %choose.1), channel_id=1, source_target_pairs={{0,2},{1,3},{2,0},{3,1},{4,6},{5,7},{6,4},{7,5},{8,10},{9,11},{10,... | collective-permute-start | bytes 196616 | tf_op jit(solution)/shard_map/ppermute | solution.py:311
  20.1 4.1 %collective-permute-start.6 = (bf16[160,128]{1,0:T(8,128)(2,1)S(1)}, bf16[160,128]{1,0:T(8,128)(2,1)S(1)}, u32[]{:S(2)}, u32[]{:S(2)}) collective-permute-start(bf16[160,128]{1,0:T(8,128)(2,1)S(1)} %project.1.q_ref), channel_id=1, source_target_pairs={{0,1},{1,0},{2,3},{3,2},{4,5},{5,4},{6,7},{7,6},{8,9},{9,8},{10,11... | collective-permute-start | bytes 122888 | tf_op jit(solution)/shard_map/ppermute | solution.py:311
  24.2 6.8 %collective-permute-start.9 = (bf16[2,160,128]{2,1,0:T(8,128)(2,1)S(1)}, bf16[2,160,128]{2,1,0:T(8,128)(2,1)S(1)}, u32[]{:S(2)}, u32[]{:S(2)}) collective-permute-start(bf16[2,160,128]{2,1,0:T(8,128)(2,1)S(1)} %get-tuple-element.45.after_ref), channel_id=1, source_target_pairs={{0,6},{1,7},{2,4},{3,5},{4,2},{5,3},{6,0},{7,1},{8,14},{9,15},{10,... | collective-permute-start | bytes 245768 | tf_op jit(solution)/shard_map/ppermute | solution.py:311
  27.0 6.5 %collective-permute-start.8 = (bf16[2,160,128]{2,1,0:T(8,128)(2,1)S(1)}, bf16[2,160,128]{2,1,0:T(8,128)(2,1)S(1)}, u32[]{:S(2)}, u32[]{:S(2)}) collective-permute-start(bf16[2,160,128]{2,1,0:T(8,128)(2,1)S(1)} %get-tuple-element.45.after_ref), channel_id=1, source_target_pairs={{0,4},{1,5},{2,6},{3,7},{4,0},{5,1},{6,2},{7,3},{8,12},{9,13},{10,... | collective-permute-start | bytes 245768 | tf_op jit(solution)/shard_map/ppermute | solution.py:311
  27.0 6.5 %collective-permute-start.7 = (bf16[2,160,128]{2,1,0:T(8,128)(2,1)S(1)}, bf16[2,160,128]{2,1,0:T(8,128)(2,1)S(1)}, u32[]{:S(2)}, u32[]{:S(2)}) collective-permute-start(bf16[2,160,128]{2,1,0:T(8,128)(2,1)S(1)} %get-tuple-element.45.after_ref), channel_id=1, source_target_pairs={{0,2},{1,3},{2,0},{3,1},{4,6},{5,7},{6,4},{7,5},{8,10},{9,11},{10,... | collective-permute-start | bytes 245768 | tf_op jit(solution)/shard_map/ppermute | solution.py:311
  36.8 7.0 %collective-permute-start.10 = (f32[136,128]{1,0:T(8,128)S(1)}, f32[136,128]{1,0:T(8,128)S(1)}, u32[]{:S(2)}, u32[]{:S(2)}) collective-permute-start(f32[136,128]{1,0:T(8,128)S(1)} %get-tuple-element.26), channel_id=1, source_target_pairs={{0,1},{1,0},{2,3},{3,2},{4,5},{5,4},{6,7},{7,6},{8,9},{9,8},{10,11... | collective-permute-start | bytes 208904 | tf_op jit(solution)/shard_map/ppermute | solution.py:311
  38.0 8.0 %collective-permute-start.11 = (f32[136,128]{1,0:T(8,128)S(1)}, f32[136,128]{1,0:T(8,128)S(1)}, u32[]{:S(2)}, u32[]{:S(2)}) collective-permute-start(f32[136,128]{1,0:T(8,128)S(1)} %get-tuple-element.27), channel_id=1, source_target_pairs={{0,2},{1,3},{2,0},{3,1},{4,6},{5,7},{6,4},{7,5},{8,10},{9,11},{10,... | collective-permute-start | bytes 208904 | tf_op jit(solution)/shard_map/ppermute | solution.py:311
  38.0 10.0 %collective-permute-start.12 = (f32[136,128]{1,0:T(8,128)S(1)}, f32[136,128]{1,0:T(8,128)S(1)}, u32[]{:S(2)}, u32[]{:S(2)}) collective-permute-start(f32[136,128]{1,0:T(8,128)S(1)} %get-tuple-element.28), channel_id=1, source_target_pairs={{0,3},{1,2},{2,1},{3,0},{4,7},{5,6},{6,5},{7,4},{8,11},{9,10},{10,... | collective-permute-start | bytes 208904 | tf_op jit(solution)/shard_map/ppermute | solution.py:311
  40.3 10.0 %collective-permute-start.13 = (f32[136,128]{1,0:T(8,128)S(1)}, f32[136,128]{1,0:T(8,128)S(1)}, u32[]{:S(2)}, u32[]{:S(2)}) collective-permute-start(f32[136,128]{1,0:T(8,128)S(1)} %get-tuple-element.29), channel_id=1, source_target_pairs={{0,4},{1,5},{2,6},{3,7},{4,0},{5,1},{6,2},{7,3},{8,12},{9,13},{10,... | collective-permute-start | bytes 208904 | tf_op jit(solution)/shard_map/ppermute | solution.py:311
  41.2 10.8 %collective-permute-start.14 = (f32[136,128]{1,0:T(8,128)S(1)}, f32[136,128]{1,0:T(8,128)S(1)}, u32[]{:S(2)}, u32[]{:S(2)}) collective-permute-start(f32[136,128]{1,0:T(8,128)S(1)} %get-tuple-element.30), channel_id=1, source_target_pairs={{0,5},{1,4},{2,7},{3,6},{4,1},{5,0},{6,3},{7,2},{8,13},{9,12},{10,... | collective-permute-start | bytes 208904 | tf_op jit(solution)/shard_map/ppermute | solution.py:311
  43.8 8.2 %collective-permute-start.15 = (f32[136,128]{1,0:T(8,128)S(1)}, f32[136,128]{1,0:T(8,128)S(1)}, u32[]{:S(2)}, u32[]{:S(2)}) collective-permute-start(f32[136,128]{1,0:T(8,128)S(1)} %get-tuple-element.31), channel_id=1, source_target_pairs={{0,6},{1,7},{2,4},{3,5},{4,2},{5,3},{6,0},{7,1},{8,14},{9,15},{10,... | collective-permute-start | bytes 208904 | tf_op jit(solution)/shard_map/ppermute | solution.py:311
  45.9 7.1 %collective-permute-start.16 = (f32[136,128]{1,0:T(8,128)S(1)}, f32[136,128]{1,0:T(8,128)S(1)}, u32[]{:S(2)}, u32[]{:S(2)}) collective-permute-start(f32[136,128]{1,0:T(8,128)S(1)} %get-tuple-element.32), channel_id=1, source_target_pairs={{0,7},{1,6},{2,5},{3,4},{4,3},{5,2},{6,1},{7,0},{8,15},{9,14},{10,... | collective-permute-start | bytes 208904 | tf_op jit(solution)/shard_map/ppermute | solution.py:311
  55.9 6.4 %collective-permute-start.17 = (f32[136,128]{1,0:T(8,128)S(1)}, f32[136,128]{1,0:T(8,128)S(1)}, u32[]{:S(2)}, u32[]{:S(2)}) collective-permute-start(f32[136,128]{1,0:T(8,128)S(1)} %get-tuple-element.34), channel_id=1, source_target_pairs={{0,1},{1,0},{2,3},{3,2},{4,5},{5,4},{6,7},{7,6},{8,9},{9,8},{10,11... | collective-permute-start | bytes 208904 | tf_op jit(solution)/shard_map/ppermute | solution.py:311
  56.4 8.0 %collective-permute-start.18 = (f32[136,128]{1,0:T(8,128)S(1)}, f32[136,128]{1,0:T(8,128)S(1)}, u32[]{:S(2)}, u32[]{:S(2)}) collective-permute-start(f32[136,128]{1,0:T(8,128)S(1)} %get-tuple-element.35), channel_id=1, source_target_pairs={{0,2},{1,3},{2,0},{3,1},{4,6},{5,7},{6,4},{7,5},{8,10},{9,11},{10,... | collective-permute-start | bytes 208904 | tf_op jit(solution)/shard_map/ppermute | solution.py:311
  58.4 8.6 %collective-permute-start.19 = (f32[136,128]{1,0:T(8,128)S(1)}, f32[136,128]{1,0:T(8,128)S(1)}, u32[]{:S(2)}, u32[]{:S(2)}) collective-permute-start(f32[136,128]{1,0:T(8,128)S(1)} %get-tuple-element.36), channel_id=1, source_target_pairs={{0,3},{1,2},{2,1},{3,0},{4,7},{5,6},{6,5},{7,4},{8,11},{9,10},{10,... | collective-permute-start | bytes 208904 | tf_op jit(solution)/shard_map/ppermute | solution.py:311
  59.4 9.7 %collective-permute-start.20 = (f32[136,128]{1,0:T(8,128)S(1)}, f32[136,128]{1,0:T(8,128)S(1)}, u32[]{:S(2)}, u32[]{:S(2)}) collective-permute-start(f32[136,128]{1,0:T(8,128)S(1)} %get-tuple-element.37), channel_id=1, source_target_pairs={{0,4},{1,5},{2,6},{3,7},{4,0},{5,1},{6,2},{7,3},{8,12},{9,13},{10,... | collective-permute-start | bytes 208904 | tf_op jit(solution)/shard_map/ppermute | solution.py:311
  61.9 9.8 %collective-permute-start.21 = (f32[136,128]{1,0:T(8,128)S(1)}, f32[136,128]{1,0:T(8,128)S(1)}, u32[]{:S(2)}, u32[]{:S(2)}) collective-permute-start(f32[136,128]{1,0:T(8,128)S(1)} %get-tuple-element.38), channel_id=1, source_target_pairs={{0,5},{1,4},{2,7},{3,6},{4,1},{5,0},{6,3},{7,2},{8,13},{9,12},{10,... | collective-permute-start | bytes 208904 | tf_op jit(solution)/shard_map/ppermute | solution.py:311
  62.3 9.4 %collective-permute-start.22 = (f32[136,128]{1,0:T(8,128)S(1)}, f32[136,128]{1,0:T(8,128)S(1)}, u32[]{:S(2)}, u32[]{:S(2)}) collective-permute-start(f32[136,128]{1,0:T(8,128)S(1)} %get-tuple-element.39), channel_id=1, source_target_pairs={{0,6},{1,7},{2,4},{3,5},{4,2},{5,3},{6,0},{7,1},{8,14},{9,15},{10,... | collective-permute-start | bytes 208904 | tf_op jit(solution)/shard_map/ppermute | solution.py:311
  64.4 7.3 %collective-permute-start.23 = (f32[136,128]{1,0:T(8,128)S(1)}, f32[136,128]{1,0:T(8,128)S(1)}, u32[]{:S(2)}, u32[]{:S(2)}) collective-permute-start(f32[136,128]{1,0:T(8,128)S(1)} %get-tuple-element.40), channel_id=1, source_target_pairs={{0,7},{1,6},{2,5},{3,4},{4,3},{5,2},{6,1},{7,0},{8,15},{9,14},{10,... | collective-permute-start | bytes 208904 | tf_op jit(solution)/shard_map/ppermute | solution.py:311
  (19 other events, 304.8 us)
where the time goes:
time: 73.9 us; the launch traced here: 73.8 us
  starting transfers between devices  35.8 us (48%)
  waiting for transfers between devices  22.5 us (30%)
  Pallas kernels  12.9 us (17%)
  between operations  0.94 us (1%)
  matrix products  0.74 us (1%)
    ppermute x22, starting transfers between devices, partner(): return lax.ppermute(x, 'tensor', [(i, i ^ bits) for i in range(chunks)])  33.2 us
    ppermute x22, waiting for transfers between devices, partner(): return lax.ppermute(x, 'tensor', [(i, i ^ bits) for i in range(chunks)])  21.9 us
    pallas_call x1, Pallas kernels, local(): pl.pallas_call(functools.partial(attend_kernel, pages, page_rows), in_spe...  3.22 us
    pallas_call x1, Pallas kernels, local(): pl.pallas_call(functools.partial(project_kernel, pages, per_page, depth),...  3.12 us
    pallas_call x1, Pallas kernels, local(): pl.pallas_call(functools.partial(merge_kernel, pages, per_page, depth, sp...  2.76 us
    ppermute x1, starting transfers between devices, local(): both = lax.ppermute(own, ('dp', 'tensor'), cross)  2.5 us
    pallas_call x1, Pallas kernels, local(): pl.pallas_call(reward_kernel, in_specs=[ANY, ANY, VMEM, VMEM] + [ANY] * 0...  2.31 us
  transfers between devices with their start and end apart: 25, of which 12 were waited for; matrix products, arithmetic and copies ran while one was open for 1% of the time, Pallas kernels for 5%

commit v1 on v0

--- a/solution.py
+++ b/solution.py
@@ -167,10 +167,10 @@
     tops, totals = [], []
     for i in range(pages):
         for r in range(KVH):
-            spread[i, r * page_rows : (r + 1) * page_rows, aligned(me ^ r, HD)] = q_ref[
+            spread[r * page_rows : (r + 1) * page_rows, aligned(me ^ r, HD)] = q_ref[
                 r, i * page_rows : (i + 1) * page_rows, :
             ]
-        scores = dot(k_ref[meta_ref[i]], spread[i], NT) * SCALE
+        scores = dot(k_ref[meta_ref[i]], spread[...], NT) * SCALE
         valid = first + iota((width, span), 0) < meta_ref[pages + i]
         scores = jnp.where(valid, scores, NEG)
         top = jnp.max(scores, axis=0, keepdims=True)
@@ -180,11 +180,11 @@
         for part in range(KVH // share):
             values = v_ref[meta_ref[i], :, aligned(part ^ lax.div(me, share), share * HD)]
             lines = slice(part * share * page_rows, (part + 1) * share * page_rows)
-            product[i, lines] = dot(weights[:, lines], values, TN)
+            product[lines] = dot(weights[:, lines], values, TN)
         for r in range(KVH):
             out = outs[r] if len(outs) > 1 else outs[0].at[r]
             out[i * page_rows : (i + 1) * page_rows, :] = product[
-                i, r * page_rows : (r + 1) * page_rows, aligned((me ^ r) & (share - 1), HD)
+                r * page_rows : (r + 1) * page_rows, aligned((me ^ r) & (share - 1), HD)
             ]
         tops.append(top)
         totals.append(total)
@@ -485,10 +485,10 @@
             else [jax.ShapeDtypeStruct((KVH,) + block, jnp.float32)]
         ),
         scratch_shapes=[
-            pltpu.VMEM((pages, KVH * page_rows, KVH * HD), jnp.bfloat16),
-            pltpu.VMEM((pages, KVH * page_rows, LANES // page_rows * HD), jnp.float32),
+            pltpu.VMEM((KVH * page_rows, KVH * HD), jnp.bfloat16),
+            pltpu.VMEM((KVH * page_rows, LANES // page_rows * HD), jnp.float32),
         ],
-        compiler_params=pltpu.CompilerParams(vmem_limit_bytes=10 * MIB),
+        compiler_params=pltpu.CompilerParams(vmem_limit_bytes=6 * MIB),
         cost_estimate=pl.CostEstimate(
             flops=4 * pages * width * KVH * HD * KVH * page_rows,
             bytes_accessed=4 * pages * width * KVH * HD,

time: 73.9 us -> 73.8 us (level)
  no operation moved by 1% of the time
where the time goes in v1:
time: 73.8 us; the launch traced here: 73.6 us
  starting transfers between devices  35.8 us (49%)
  waiting for transfers between devices  22.5 us (30%)
  Pallas kernels  12.8 us (17%)
  between operations  0.94 us (1%)
  matrix products  0.74 us (1%)
    ppermute x22, starting transfers between devices, partner(): return lax.ppermute(x, 'tensor', [(i, i ^ bits) for i in range(chunks)])  33.2 us
    ppermute x22, waiting for transfers between devices, partner(): return lax.ppermute(x, 'tensor', [(i, i ^ bits) for i in range(chunks)])  21.9 us
    pallas_call x1, Pallas kernels, local(): pl.pallas_call(functools.partial(project_kernel, pages, per_page, depth),...  3.12 us
    pallas_call x1, Pallas kernels, local(): pl.pallas_call(functools.partial(attend_kernel, pages, page_rows), in_spe...  3.08 us
    pallas_call x1, Pallas kernels, local(): pl.pallas_call(functools.partial(merge_kernel, pages, per_page, depth, sp...  2.76 us
    ppermute x1, starting transfers between devices, local(): both = lax.ppermute(own, ('dp', 'tensor'), cross)  2.5 us
    pallas_call x1, Pallas kernels, local(): pl.pallas_call(reward_kernel, in_specs=[ANY, ANY, VMEM, VMEM] + [ANY] * 0...  2.31 us
  transfers between devices with their start and end apart: 25, of which 12 were waited for; matrix products, arithmetic and copies ran while one was open for 1% of the time, Pallas kernels for 5%

profile of v1, /device:TPU:0, one launch (start us, length us, event | category | flops | bytes accessed | tf_op | source)
XLA Modules:
  0.0 73.6 jit_solution(4858373334423860076)
XLA Ops:
  0.7 2.5 %collective-permute-start.2 = (bf16[16,1024]{1,0:T(8,128)(2,1)}, bf16[16,1024]{1,0:T(8,128)(2,1)S(1)}, u32[]{:S(2)}, u32[]{:S(2)}) collective-permute-start(bf16[16,1024]{1,0:T(8,128)(2,1)} %bitcast.30), channel_id=1, source_target_pairs={{0,9},{1,8},{2,11},{3,10},{4,13},{5,12},{6,15},{7,14},{8,1},{9,0},... | collective-permute-start | bytes 98312 | tf_op jit(solution)/shard_map/ppermute | solution.py:399
  5.3 2.1 %collective-permute-done.1.near_ref = bf16[16,1024]{1,0:T(8,128)(2,1)S(1)} collective-permute-done((bf16[16,1024]{1,0:T(8,128)(2,1)}, bf16[16,1024]{1,0:T(8,128)(2,1)S(1)}, u32[]{:S(2)}, u32[]{:S(2)}) %collective-permute-start.1) | collective-permute-done | bytes 32800 | tf_op jit(solution)/shard_map/ppermute | solution.py:311
  7.6 3.7 %collective-permute-start.5 = (bf16[2,16,1024]{2,1,0:T(8,128)(2,1)S(1)}, bf16[2,16,1024]{2,1,0:T(8,128)(2,1)S(1)}, u32[]{:S(2)}, u32[]{:S(2)}) collective-permute-start(bf16[2,16,1024]{2,1,0:T(8,128)(2,1)S(1)} %choose.1), channel_id=1, source_target_pairs={{0,6},{1,7},{2,4},{3,5},{4,2},{5,3},{6,0},{7,1},{8,14},{9,15},{10,... | collective-permute-start | bytes 196616 | tf_op jit(solution)/shard_map/ppermute | solution.py:311
  12.0 2.1 %collective-permute-done.5 = bf16[2,16,1024]{2,1,0:T(8,128)(2,1)S(1)} collective-permute-done((bf16[2,16,1024]{2,1,0:T(8,128)(2,1)S(1)}, bf16[2,16,1024]{2,1,0:T(8,128)(2,1)S(1)}, u32[]{:S(2)}, u32[]{:S(2)}) %collective-permute-start.5) | collective-permute-done | bytes 65568 | tf_op jit(solution)/shard_map/ppermute | solution.py:311
  14.1 2.7 %collective-permute-done.4 = bf16[2,16,1024]{2,1,0:T(8,128)(2,1)S(1)} collective-permute-done((bf16[2,16,1024]{2,1,0:T(8,128)(2,1)S(1)}, bf16[2,16,1024]{2,1,0:T(8,128)(2,1)S(1)}, u32[]{:S(2)}, u32[]{:S(2)}) %collective-permute-start.4) | collective-permute-done | bytes 65568 | tf_op jit(solution)/shard_map/ppermute | solution.py:311
  17.0 3.1 %project.1.q_ref = bf16[160,128]{1,0:T(8,128)(2,1)S(1)} custom-call(bf16[8,16,1024]{2,1,0:T(8,128)(2,1)S(1)} %bitcast.26, f32[8,1,1024]{2,1,0:T(1,128)S(1)} %bitcast.29, bf16[8192,1024]{1,0:T(8,128)(2,1)S(1)} %bitcast.23, bf16[8192,256]{1,0:T(8,128)(2,1)S(1)} %copy-done), custom_call_target="tpu_custom_call" | custom-call | flops 335544320 | bytes 20971520 | tf_op jit(solution)/shard_map/project/pallas_call | solution.py:415
  21.5 2.7 %collective-permute-done.6 = bf16[160,128]{1,0:T(8,128)(2,1)S(1)} collective-permute-done((bf16[160,128]{1,0:T(8,128)(2,1)S(1)}, bf16[160,128]{1,0:T(8,128)(2,1)S(1)}, u32[]{:S(2)}, u32[]{:S(2)}) %collective-permute-start.6) | collective-permute-done | bytes 40992 | tf_op jit(solution)/shard_map/ppermute | solution.py:311
  24.2 2.8 %collective-permute-start.9 = (bf16[2,160,128]{2,1,0:T(8,128)(2,1)S(1)}, bf16[2,160,128]{2,1,0:T(8,128)(2,1)S(1)}, u32[]{:S(2)}, u32[]{:S(2)}) collective-permute-start(bf16[2,160,128]{2,1,0:T(8,128)(2,1)S(1)} %get-tuple-element.45.after_ref), channel_id=1, source_target_pairs={{0,6},{1,7},{2,4},{3,5},{4,2},{5,3},{6,0},{7,1},{8,14},{9,15},{10,... | collective-permute-start | bytes 245768 | tf_op jit(solution)/shard_map/ppermute | solution.py:311
  28.7 2.3 %reward.1.reward_ref = f32[8,4,128]{2,1,0:T(4,128)S(1)} custom-call(bf16[2,160,128]{2,1,0:T(8,128)(2,1)S(1)} %get-tuple-element.45.after_ref, bf16[8,256,1024]{2,1,0:T(8,128)(2,1)S(1)} %copy-done.1, f32[1,1024]{1,0:T(1,128)S(1)} %bitcast.34, f32[1,1024]{1,0:T(1,128)S(1)} %bitcast.35), custom_call_target="tpu_custom_call" | custom-call | flops 8388608 | bytes 4194304 | tf_op jit(solution)/shard_map/reward/pallas_call | solution.py:432
  31.0 2.5 %collective-permute-done.8 = bf16[2,160,128]{2,1,0:T(8,128)(2,1)S(1)} collective-permute-done((bf16[2,160,128]{2,1,0:T(8,128)(2,1)S(1)}, bf16[2,160,128]{2,1,0:T(8,128)(2,1)S(1)}, u32[]{:S(2)}, u32[]{:S(2)}) %collective-permute-start.8) | collective-permute-done | bytes 81952 | tf_op jit(solution)/shard_map/ppermute | solution.py:311
  33.5 3.1 %attend.1 = (f32[136,128]{1,0:T(8,128)S(1)}, f32[136,128]{1,0:T(8,128)S(1)}, f32[136,128]{1,0:T(8,128)S(1)}, f32[136,128]{1,0:T(8,128)S(1)}, f32[136,128]{1,0:T(...) custom-call(s32[8]{0:T(128)S(1)} %get-tuple-element.24.meta_ref, ...), custom_call_target="tpu_custom_call" | custom-call | flops 1073741824 | bytes 4194304 | tf_op jit(solution)/shard_map/attend/pallas_call | solution.py:478
  37.8 2.4 %collective-permute-start.12 = (f32[136,128]{1,0:T(8,128)S(1)}, f32[136,128]{1,0:T(8,128)S(1)}, u32[]{:S(2)}, u32[]{:S(2)}) collective-permute-start(f32[136,128]{1,0:T(8,128)S(1)} %get-tuple-element.28), channel_id=1, source_target_pairs={{0,3},{1,2},{2,1},{3,0},{4,7},{5,6},{6,5},{7,4},{8,11},{9,10},{10,... | collective-permute-start | bytes 208904 | tf_op jit(solution)/shard_map/ppermute | solution.py:311
  41.1 2.6 %collective-permute-start.14 = (f32[136,128]{1,0:T(8,128)S(1)}, f32[136,128]{1,0:T(8,128)S(1)}, u32[]{:S(2)}, u32[]{:S(2)}) collective-permute-start(f32[136,128]{1,0:T(8,128)S(1)} %get-tuple-element.30), channel_id=1, source_target_pairs={{0,5},{1,4},{2,7},{3,6},{4,1},{5,0},{6,3},{7,2},{8,13},{9,12},{10,... | collective-permute-start | bytes 208904 | tf_op jit(solution)/shard_map/ppermute | solution.py:311
  43.7 2.1 %collective-permute-start.15 = (f32[136,128]{1,0:T(8,128)S(1)}, f32[136,128]{1,0:T(8,128)S(1)}, u32[]{:S(2)}, u32[]{:S(2)}) collective-permute-start(f32[136,128]{1,0:T(8,128)S(1)} %get-tuple-element.31), channel_id=1, source_target_pairs={{0,6},{1,7},{2,4},{3,5},{4,2},{5,3},{6,0},{7,1},{8,14},{9,15},{10,... | collective-permute-start | bytes 208904 | tf_op jit(solution)/shard_map/ppermute | solution.py:311
  45.8 2.0 %collective-permute-start.16 = (f32[136,128]{1,0:T(8,128)S(1)}, f32[136,128]{1,0:T(8,128)S(1)}, u32[]{:S(2)}, u32[]{:S(2)}) collective-permute-start(f32[136,128]{1,0:T(8,128)S(1)} %get-tuple-element.32), channel_id=1, source_target_pairs={{0,7},{1,6},{2,5},{3,4},{4,3},{5,2},{6,1},{7,0},{8,15},{9,14},{10,... | collective-permute-start | bytes 208904 | tf_op jit(solution)/shard_map/ppermute | solution.py:311
  47.8 2.3 %collective-permute-done.13.rest_4_ = f32[136,128]{1,0:T(8,128)S(1)} collective-permute-done((f32[136,128]{1,0:T(8,128)S(1)}, f32[136,128]{1,0:T(8,128)S(1)}, u32[]{:S(2)}, u32[]{:S(2)}) %collective-permute-start.13) | collective-permute-done | bytes 69664 | tf_op jit(solution)/shard_map/ppermute | solution.py:311
  50.1 1.8 %collective-permute-done.14.rest_5_ = f32[136,128]{1,0:T(8,128)S(1)} collective-permute-done((f32[136,128]{1,0:T(8,128)S(1)}, f32[136,128]{1,0:T(8,128)S(1)}, u32[]{:S(2)}, u32[]{:S(2)}) %collective-permute-start.14) | collective-permute-done | bytes 69664 | tf_op jit(solution)/shard_map/ppermute | solution.py:311
  52.9 2.8 %merge.1 = (f32[136,128]{1,0:T(8,128)S(1)}, f32[136,128]{1,0:T(8,128)S(1)}, f32[136,128]{1,0:T(8,128)S(1)}, f32[136,128]{1,0:T(8,128)S(1)}, f32[136,128]{1,0:T(8...) custom-call(bf16[160,128]{1,0:T(8,128)(2,1)S(1)} %project.1.q_ref, ...), custom_call_target="tpu_custom_call" | custom-call | flops 268435456 | bytes 16777216 | tf_op jit(solution)/shard_map/merge/pallas_call | solution.py:513
  56.3 2.0 %collective-permute-start.18 = (f32[136,128]{1,0:T(8,128)S(1)}, f32[136,128]{1,0:T(8,128)S(1)}, u32[]{:S(2)}, u32[]{:S(2)}) collective-permute-start(f32[136,128]{1,0:T(8,128)S(1)} %get-tuple-element.35), channel_id=1, source_target_pairs={{0,2},{1,3},{2,0},{3,1},{4,6},{5,7},{6,4},{7,5},{8,10},{9,11},{10,... | collective-permute-start | bytes 208904 | tf_op jit(solution)/shard_map/ppermute | solution.py:311
  59.2 2.6 %collective-permute-start.20 = (f32[136,128]{1,0:T(8,128)S(1)}, f32[136,128]{1,0:T(8,128)S(1)}, u32[]{:S(2)}, u32[]{:S(2)}) collective-permute-start(f32[136,128]{1,0:T(8,128)S(1)} %get-tuple-element.37), channel_id=1, source_target_pairs={{0,4},{1,5},{2,6},{3,7},{4,0},{5,1},{6,2},{7,3},{8,12},{9,13},{10,... | collective-permute-start | bytes 208904 | tf_op jit(solution)/shard_map/ppermute | solution.py:311
  62.1 2.1 %collective-permute-start.22 = (f32[136,128]{1,0:T(8,128)S(1)}, f32[136,128]{1,0:T(8,128)S(1)}, u32[]{:S(2)}, u32[]{:S(2)}) collective-permute-start(f32[136,128]{1,0:T(8,128)S(1)} %get-tuple-element.39), channel_id=1, source_target_pairs={{0,6},{1,7},{2,4},{3,5},{4,2},{5,3},{6,0},{7,1},{8,14},{9,15},{10,... | collective-permute-start | bytes 208904 | tf_op jit(solution)/shard_map/ppermute | solution.py:311
  64.2 2.6 %collective-permute-start.23 = (f32[136,128]{1,0:T(8,128)S(1)}, f32[136,128]{1,0:T(8,128)S(1)}, u32[]{:S(2)}, u32[]{:S(2)}) collective-permute-start(f32[136,128]{1,0:T(8,128)S(1)} %get-tuple-element.40), channel_id=1, source_target_pairs={{0,7},{1,6},{2,5},{3,4},{4,3},{5,2},{6,1},{7,0},{8,15},{9,14},{10,... | collective-permute-start | bytes 208904 | tf_op jit(solution)/shard_map/ppermute | solution.py:311
  66.9 2.0 %collective-permute-done.20.refs_4_ = f32[136,128]{1,0:T(8,128)S(1)} collective-permute-done((f32[136,128]{1,0:T(8,128)S(1)}, f32[136,128]{1,0:T(8,128)S(1)}, u32[]{:S(2)}, u32[]{:S(2)}) %collective-permute-start.20) | collective-permute-done | bytes 69664 | tf_op jit(solution)/shard_map/ppermute | solution.py:311
  68.9 2.7 %collective-permute-done.21.refs_5_ = f32[136,128]{1,0:T(8,128)S(1)} collective-permute-done((f32[136,128]{1,0:T(8,128)S(1)}, f32[136,128]{1,0:T(8,128)S(1)}, u32[]{:S(2)}, u32[]{:S(2)}) %collective-permute-start.21) | collective-permute-done | bytes 69664 | tf_op jit(solution)/shard_map/ppermute | solution.py:311
  (77 shorter events, 13.2 us)
Async XLA Ops:
  0.7 4.6 %collective-permute-start.2 = (bf16[16,1024]{1,0:T(8,128)(2,1)}, bf16[16,1024]{1,0:T(8,128)(2,1)S(1)}, u32[]{:S(2)}, u32[]{:S(2)}) collective-permute-start(bf16[16,1024]{1,0:T(8,128)(2,1)} %bitcast.30), channel_id=1, source_target_pairs={{0,9},{1,8},{2,11},{3,10},{4,13},{5,12},{6,15},{7,14},{8,1},{9,0},... | collective-permute-start | bytes 98312 | tf_op jit(solution)/shard_map/ppermute | solution.py:399
  3.2 4.2 %collective-permute-start.1 = (bf16[16,1024]{1,0:T(8,128)(2,1)}, bf16[16,1024]{1,0:T(8,128)(2,1)S(1)}, u32[]{:S(2)}, u32[]{:S(2)}) collective-permute-start(bf16[16,1024]{1,0:T(8,128)(2,1)} %bitcast.31), channel_id=1, source_target_pairs={{0,1},{1,0},{2,3},{3,2},{4,5},{5,4},{6,7},{7,6},{8,9},{9,8},{10,11... | collective-permute-start | bytes 98312 | tf_op jit(solution)/shard_map/ppermute | solution.py:311
  3.9 3.5 %collective-permute-start = (bf16[16,1024]{1,0:T(8,128)(2,1)}, bf16[16,1024]{1,0:T(8,128)(2,1)S(1)}, u32[]{:S(2)}, u32[]{:S(2)}) collective-permute-start(bf16[16,1024]{1,0:T(8,128)(2,1)} %bitcast.32), channel_id=1, source_target_pairs={{0,8},{8,0},{1,9},{9,1},{2,10},{10,2},{3,11},{11,3},{4,12},{12,4},... | collective-permute-start | bytes 98312 | tf_op jit(solution)/shard_map/ppermute | solution.py:393
  7.6 6.6 %collective-permute-start.5 = (bf16[2,16,1024]{2,1,0:T(8,128)(2,1)S(1)}, bf16[2,16,1024]{2,1,0:T(8,128)(2,1)S(1)}, u32[]{:S(2)}, u32[]{:S(2)}) collective-permute-start(bf16[2,16,1024]{2,1,0:T(8,128)(2,1)S(1)} %choose.1), channel_id=1, source_target_pairs={{0,6},{1,7},{2,4},{3,5},{4,2},{5,3},{6,0},{7,1},{8,14},{9,15},{10,... | collective-permute-start | bytes 196616 | tf_op jit(solution)/shard_map/ppermute | solution.py:311
  11.2 5.6 %collective-permute-start.4 = (bf16[2,16,1024]{2,1,0:T(8,128)(2,1)S(1)}, bf16[2,16,1024]{2,1,0:T(8,128)(2,1)S(1)}, u32[]{:S(2)}, u32[]{:S(2)}) collective-permute-start(bf16[2,16,1024]{2,1,0:T(8,128)(2,1)S(1)} %choose.1), channel_id=1, source_target_pairs={{0,4},{1,5},{2,6},{3,7},{4,0},{5,1},{6,2},{7,3},{8,12},{9,13},{10,... | collective-permute-start | bytes 196616 | tf_op jit(solution)/shard_map/ppermute | solution.py:311
  11.2 5.6 %collective-permute-start.3 = (bf16[2,16,1024]{2,1,0:T(8,128)(2,1)S(1)}, bf16[2,16,1024]{2,1,0:T(8,128)(2,1)S(1)}, u32[]{:S(2)}, u32[]{:S(2)}) collective-permute-start(bf16[2,16,1024]{2,1,0:T(8,128)(2,1)S(1)} %choose.1), channel_id=1, source_target_pairs={{0,2},{1,3},{2,0},{3,1},{4,6},{5,7},{6,4},{7,5},{8,10},{9,11},{10,... | collective-permute-start | bytes 196616 | tf_op jit(solution)/shard_map/ppermute | solution.py:311
  20.1 4.1 %collective-permute-start.6 = (bf16[160,128]{1,0:T(8,128)(2,1)S(1)}, bf16[160,128]{1,0:T(8,128)(2,1)S(1)}, u32[]{:S(2)}, u32[]{:S(2)}) collective-permute-start(bf16[160,128]{1,0:T(8,128)(2,1)S(1)} %project.1.q_ref), channel_id=1, source_target_pairs={{0,1},{1,0},{2,3},{3,2},{4,5},{5,4},{6,7},{7,6},{8,9},{9,8},{10,11... | collective-permute-start | bytes 122888 | tf_op jit(solution)/shard_map/ppermute | solution.py:311
  24.2 6.8 %collective-permute-start.9 = (bf16[2,160,128]{2,1,0:T(8,128)(2,1)S(1)}, bf16[2,160,128]{2,1,0:T(8,128)(2,1)S(1)}, u32[]{:S(2)}, u32[]{:S(2)}) collective-permute-start(bf16[2,160,128]{2,1,0:T(8,128)(2,1)S(1)} %get-tuple-element.45.after_ref), channel_id=1, source_target_pairs={{0,6},{1,7},{2,4},{3,5},{4,2},{5,3},{6,0},{7,1},{8,14},{9,15},{10,... | collective-permute-start | bytes 245768 | tf_op jit(solution)/shard_map/ppermute | solution.py:311
  27.0 6.5 %collective-permute-start.8 = (bf16[2,160,128]{2,1,0:T(8,128)(2,1)S(1)}, bf16[2,160,128]{2,1,0:T(8,128)(2,1)S(1)}, u32[]{:S(2)}, u32[]{:S(2)}) collective-permute-start(bf16[2,160,128]{2,1,0:T(8,128)(2,1)S(1)} %get-tuple-element.45.after_ref), channel_id=1, source_target_pairs={{0,4},{1,5},{2,6},{3,7},{4,0},{5,1},{6,2},{7,3},{8,12},{9,13},{10,... | collective-permute-start | bytes 245768 | tf_op jit(solution)/shard_map/ppermute | solution.py:311
  27.0 6.5 %collective-permute-start.7 = (bf16[2,160,128]{2,1,0:T(8,128)(2,1)S(1)}, bf16[2,160,128]{2,1,0:T(8,128)(2,1)S(1)}, u32[]{:S(2)}, u32[]{:S(2)}) collective-permute-start(bf16[2,160,128]{2,1,0:T(8,128)(2,1)S(1)} %get-tuple-element.45.after_ref), channel_id=1, source_target_pairs={{0,2},{1,3},{2,0},{3,1},{4,6},{5,7},{6,4},{7,5},{8,10},{9,11},{10,... | collective-permute-start | bytes 245768 | tf_op jit(solution)/shard_map/ppermute | solution.py:311
  36.6 7.0 %collective-permute-start.10 = (f32[136,128]{1,0:T(8,128)S(1)}, f32[136,128]{1,0:T(8,128)S(1)}, u32[]{:S(2)}, u32[]{:S(2)}) collective-permute-start(f32[136,128]{1,0:T(8,128)S(1)} %get-tuple-element.26), channel_id=1, source_target_pairs={{0,1},{1,0},{2,3},{3,2},{4,5},{5,4},{6,7},{7,6},{8,9},{9,8},{10,11... | collective-permute-start | bytes 208904 | tf_op jit(solution)/shard_map/ppermute | solution.py:311
  37.8 8.0 %collective-permute-start.11 = (f32[136,128]{1,0:T(8,128)S(1)}, f32[136,128]{1,0:T(8,128)S(1)}, u32[]{:S(2)}, u32[]{:S(2)}) collective-permute-start(f32[136,128]{1,0:T(8,128)S(1)} %get-tuple-element.27), channel_id=1, source_target_pairs={{0,2},{1,3},{2,0},{3,1},{4,6},{5,7},{6,4},{7,5},{8,10},{9,11},{10,... | collective-permute-start | bytes 208904 | tf_op jit(solution)/shard_map/ppermute | solution.py:311
  37.8 10.0 %collective-permute-start.12 = (f32[136,128]{1,0:T(8,128)S(1)}, f32[136,128]{1,0:T(8,128)S(1)}, u32[]{:S(2)}, u32[]{:S(2)}) collective-permute-start(f32[136,128]{1,0:T(8,128)S(1)} %get-tuple-element.28), channel_id=1, source_target_pairs={{0,3},{1,2},{2,1},{3,0},{4,7},{5,6},{6,5},{7,4},{8,11},{9,10},{10,... | collective-permute-start | bytes 208904 | tf_op jit(solution)/shard_map/ppermute | solution.py:311
  40.2 10.0 %collective-permute-start.13 = (f32[136,128]{1,0:T(8,128)S(1)}, f32[136,128]{1,0:T(8,128)S(1)}, u32[]{:S(2)}, u32[]{:S(2)}) collective-permute-start(f32[136,128]{1,0:T(8,128)S(1)} %get-tuple-element.29), channel_id=1, source_target_pairs={{0,4},{1,5},{2,6},{3,7},{4,0},{5,1},{6,2},{7,3},{8,12},{9,13},{10,... | collective-permute-start | bytes 208904 | tf_op jit(solution)/shard_map/ppermute | solution.py:311
  41.1 10.8 %collective-permute-start.14 = (f32[136,128]{1,0:T(8,128)S(1)}, f32[136,128]{1,0:T(8,128)S(1)}, u32[]{:S(2)}, u32[]{:S(2)}) collective-permute-start(f32[136,128]{1,0:T(8,128)S(1)} %get-tuple-element.30), channel_id=1, source_target_pairs={{0,5},{1,4},{2,7},{3,6},{4,1},{5,0},{6,3},{7,2},{8,13},{9,12},{10,... | collective-permute-start | bytes 208904 | tf_op jit(solution)/shard_map/ppermute | solution.py:311
  43.7 8.2 %collective-permute-start.15 = (f32[136,128]{1,0:T(8,128)S(1)}, f32[136,128]{1,0:T(8,128)S(1)}, u32[]{:S(2)}, u32[]{:S(2)}) collective-permute-start(f32[136,128]{1,0:T(8,128)S(1)} %get-tuple-element.31), channel_id=1, source_target_pairs={{0,6},{1,7},{2,4},{3,5},{4,2},{5,3},{6,0},{7,1},{8,14},{9,15},{10,... | collective-permute-start | bytes 208904 | tf_op jit(solution)/shard_map/ppermute | solution.py:311
  45.8 7.1 %collective-permute-start.16 = (f32[136,128]{1,0:T(8,128)S(1)}, f32[136,128]{1,0:T(8,128)S(1)}, u32[]{:S(2)}, u32[]{:S(2)}) collective-permute-start(f32[136,128]{1,0:T(8,128)S(1)} %get-tuple-element.32), channel_id=1, source_target_pairs={{0,7},{1,6},{2,5},{3,4},{4,3},{5,2},{6,1},{7,0},{8,15},{9,14},{10,... | collective-permute-start | bytes 208904 | tf_op jit(solution)/shard_map/ppermute | solution.py:311
  55.7 6.4 %collective-permute-start.17 = (f32[136,128]{1,0:T(8,128)S(1)}, f32[136,128]{1,0:T(8,128)S(1)}, u32[]{:S(2)}, u32[]{:S(2)}) collective-permute-start(f32[136,128]{1,0:T(8,128)S(1)} %get-tuple-element.34), channel_id=1, source_target_pairs={{0,1},{1,0},{2,3},{3,2},{4,5},{5,4},{6,7},{7,6},{8,9},{9,8},{10,11... | collective-permute-start | bytes 208904 | tf_op jit(solution)/shard_map/ppermute | solution.py:311
  56.3 8.0 %collective-permute-start.18 = (f32[136,128]{1,0:T(8,128)S(1)}, f32[136,128]{1,0:T(8,128)S(1)}, u32[]{:S(2)}, u32[]{:S(2)}) collective-permute-start(f32[136,128]{1,0:T(8,128)S(1)} %get-tuple-element.35), channel_id=1, source_target_pairs={{0,2},{1,3},{2,0},{3,1},{4,6},{5,7},{6,4},{7,5},{8,10},{9,11},{10,... | collective-permute-start | bytes 208904 | tf_op jit(solution)/shard_map/ppermute | solution.py:311
  58.3 8.6 %collective-permute-start.19 = (f32[136,128]{1,0:T(8,128)S(1)}, f32[136,128]{1,0:T(8,128)S(1)}, u32[]{:S(2)}, u32[]{:S(2)}) collective-permute-start(f32[136,128]{1,0:T(8,128)S(1)} %get-tuple-element.36), channel_id=1, source_target_pairs={{0,3},{1,2},{2,1},{3,0},{4,7},{5,6},{6,5},{7,4},{8,11},{9,10},{10,... | collective-permute-start | bytes 208904 | tf_op jit(solution)/shard_map/ppermute | solution.py:311
  59.2 9.7 %collective-permute-start.20 = (f32[136,128]{1,0:T(8,128)S(1)}, f32[136,128]{1,0:T(8,128)S(1)}, u32[]{:S(2)}, u32[]{:S(2)}) collective-permute-start(f32[136,128]{1,0:T(8,128)S(1)} %get-tuple-element.37), channel_id=1, source_target_pairs={{0,4},{1,5},{2,6},{3,7},{4,0},{5,1},{6,2},{7,3},{8,12},{9,13},{10,... | collective-permute-start | bytes 208904 | tf_op jit(solution)/shard_map/ppermute | solution.py:311
  61.8 9.8 %collective-permute-start.21 = (f32[136,128]{1,0:T(8,128)S(1)}, f32[136,128]{1,0:T(8,128)S(1)}, u32[]{:S(2)}, u32[]{:S(2)}) collective-permute-start(f32[136,128]{1,0:T(8,128)S(1)} %get-tuple-element.38), channel_id=1, source_target_pairs={{0,5},{1,4},{2,7},{3,6},{4,1},{5,0},{6,3},{7,2},{8,13},{9,12},{10,... | collective-permute-start | bytes 208904 | tf_op jit(solution)/shard_map/ppermute | solution.py:311
  62.1 9.4 %collective-permute-start.22 = (f32[136,128]{1,0:T(8,128)S(1)}, f32[136,128]{1,0:T(8,128)S(1)}, u32[]{:S(2)}, u32[]{:S(2)}) collective-permute-start(f32[136,128]{1,0:T(8,128)S(1)} %get-tuple-element.39), channel_id=1, source_target_pairs={{0,6},{1,7},{2,4},{3,5},{4,2},{5,3},{6,0},{7,1},{8,14},{9,15},{10,... | collective-permute-start | bytes 208904 | tf_op jit(solution)/shard_map/ppermute | solution.py:311
  64.2 7.3 %collective-permute-start.23 = (f32[136,128]{1,0:T(8,128)S(1)}, f32[136,128]{1,0:T(8,128)S(1)}, u32[]{:S(2)}, u32[]{:S(2)}) collective-permute-start(f32[136,128]{1,0:T(8,128)S(1)} %get-tuple-element.40), channel_id=1, source_target_pairs={{0,7},{1,6},{2,5},{3,4},{4,3},{5,2},{6,1},{7,0},{8,15},{9,14},{10,... | collective-permute-start | bytes 208904 | tf_op jit(solution)/shard_map/ppermute | solution.py:311
  (19 other events, 304.2 us)

commit v2 on v1

--- a/solution.py
+++ b/solution.py
@@ -164,7 +164,7 @@
     me = lax.axis_index("tensor") if len(outs) > 1 else 0
     spread[...] = jnp.zeros_like(spread)
     share = LANES // page_rows
-    tops, totals = [], []
+    stats = [[jnp.zeros((1, LANES), jnp.float32)] * 2 for _ in range(KVH)]
     for i in range(pages):
         for r in range(KVH):
             spread[r * page_rows : (r + 1) * page_rows, aligned(me ^ r, HD)] = q_ref[
@@ -186,24 +186,18 @@
             out[i * page_rows : (i + 1) * page_rows, :] = product[
                 r * page_rows : (r + 1) * page_rows, aligned((me ^ r) & (share - 1), HD)
             ]
-        tops.append(top)
-        totals.append(total)
-    held = iota((1, LANES), 1) // page_rows
-    stats = []
-    for part in range(KVH // share):
-        lanes = slice(part * LANES, (part + 1) * LANES)
-        tile = jnp.concatenate([x[:, lanes] for x in tops + totals], axis=0)
-        turned = [tile] + [pltpu.roll(tile, t * page_rows, 1) for t in range(1, share)]
-        for q in range(share):
-            for skip in (0, pages):
-                line = jnp.zeros((1, LANES), jnp.float32)
-                for i in range(pages):
-                    row = turned[(i - q) % share][skip + i : skip + i + 1]
-                    line = jnp.where(held == i, row, line)
-                stats.append(line)
+            start = r * page_rows
+            lane = start // LANES * LANES
+            shift = (i * page_rows - start) % LANES
+            mask = iota((1, LANES), 1) // page_rows == i
+            for k, packed in enumerate((top, total)):
+                packed = packed[:, lane : lane + LANES]
+                if shift:
+                    packed = pltpu.roll(packed, shift, 1)
+                stats[r][k] = jnp.where(mask, packed, stats[r][k])
     for r in range(KVH):
         out = outs[r] if len(outs) > 1 else outs[0].at[r]
-        out[body : body + 2, :] = jnp.concatenate(stats[2 * r : 2 * r + 2], axis=0)
+        out[body : body + 2, :] = jnp.concatenate(stats[r], axis=0)
         if len(outs) > 1:
             out[body + 2 : body + 4, :] = jnp.zeros((2, LANES), jnp.float32)
             out[body + 4 :, :] = reward_ref[me ^ r]

time: 73.8 us -> 73.8 us (level)
  no operation moved by 1% of the time
where the time goes in v2:
time: 73.8 us; the launch traced here: 73.6 us
  starting transfers between devices  35.8 us (49%)
  waiting for transfers between devices  22.5 us (30%)
  Pallas kernels  12.8 us (17%)
  between operations  0.94 us (1%)
  matrix products  0.74 us (1%)
    ppermute x22, starting transfers between devices, partner(): return lax.ppermute(x, 'tensor', [(i, i ^ bits) for i in range(chunks)])  33.2 us
    ppermute x22, waiting for transfers between devices, partner(): return lax.ppermute(x, 'tensor', [(i, i ^ bits) for i in range(chunks)])  21.9 us
    pallas_call x1, Pallas kernels, local(): pl.pallas_call(functools.partial(project_kernel, pages, per_page, depth),...  3.12 us
    pallas_call x1, Pallas kernels, local(): pl.pallas_call(functools.partial(attend_kernel, pages, page_rows), in_spe...  3.08 us
    pallas_call x1, Pallas kernels, local(): pl.pallas_call(functools.partial(merge_kernel, pages, per_page, depth, sp...  2.76 us
    ppermute x1, starting transfers between devices, local(): both = lax.ppermute(own, ('dp', 'tensor'), cross)  2.5 us
    pallas_call x1, Pallas kernels, local(): pl.pallas_call(reward_kernel, in_specs=[ANY, ANY, VMEM, VMEM] + [ANY] * 0...  2.31 us
  transfers between devices with their start and end apart: 25, of which 12 were waited for; matrix products, arithmetic and copies ran while one was open for 1% of the time, Pallas kernels for 5%

profile of v2, /device:TPU:0, one launch (start us, length us, event | category | flops | bytes accessed | tf_op | source)
XLA Modules:
  0.0 73.6 jit_solution(601101242383382406)
XLA Ops:
  0.7 2.5 %collective-permute-start.2 = (bf16[16,1024]{1,0:T(8,128)(2,1)}, bf16[16,1024]{1,0:T(8,128)(2,1)S(1)}, u32[]{:S(2)}, u32[]{:S(2)}) collective-permute-start(bf16[16,1024]{1,0:T(8,128)(2,1)} %bitcast.30), channel_id=1, source_target_pairs={{0,9},{1,8},{2,11},{3,10},{4,13},{5,12},{6,15},{7,14},{8,1},{9,0},... | collective-permute-start | bytes 98312 | tf_op jit(solution)/shard_map/ppermute | solution.py:393
  5.3 2.1 %collective-permute-done.1.near_ref = bf16[16,1024]{1,0:T(8,128)(2,1)S(1)} collective-permute-done((bf16[16,1024]{1,0:T(8,128)(2,1)}, bf16[16,1024]{1,0:T(8,128)(2,1)S(1)}, u32[]{:S(2)}, u32[]{:S(2)}) %collective-permute-start.1) | collective-permute-done | bytes 32800 | tf_op jit(solution)/shard_map/ppermute | solution.py:305
  7.6 3.7 %collective-permute-start.5 = (bf16[2,16,1024]{2,1,0:T(8,128)(2,1)S(1)}, bf16[2,16,1024]{2,1,0:T(8,128)(2,1)S(1)}, u32[]{:S(2)}, u32[]{:S(2)}) collective-permute-start(bf16[2,16,1024]{2,1,0:T(8,128)(2,1)S(1)} %choose.1), channel_id=1, source_target_pairs={{0,6},{1,7},{2,4},{3,5},{4,2},{5,3},{6,0},{7,1},{8,14},{9,15},{10,... | collective-permute-start | bytes 196616 | tf_op jit(solution)/shard_map/ppermute | solution.py:305
  12.0 2.1 %collective-permute-done.5 = bf16[2,16,1024]{2,1,0:T(8,128)(2,1)S(1)} collective-permute-done((bf16[2,16,1024]{2,1,0:T(8,128)(2,1)S(1)}, bf16[2,16,1024]{2,1,0:T(8,128)(2,1)S(1)}, u32[]{:S(2)}, u32[]{:S(2)}) %collective-permute-start.5) | collective-permute-done | bytes 65568 | tf_op jit(solution)/shard_map/ppermute | solution.py:305
  14.1 2.7 %collective-permute-done.4 = bf16[2,16,1024]{2,1,0:T(8,128)(2,1)S(1)} collective-permute-done((bf16[2,16,1024]{2,1,0:T(8,128)(2,1)S(1)}, bf16[2,16,1024]{2,1,0:T(8,128)(2,1)S(1)}, u32[]{:S(2)}, u32[]{:S(2)}) %collective-permute-start.4) | collective-permute-done | bytes 65568 | tf_op jit(solution)/shard_map/ppermute | solution.py:305
  17.0 3.1 %project.1.q_ref = bf16[160,128]{1,0:T(8,128)(2,1)S(1)} custom-call(bf16[8,16,1024]{2,1,0:T(8,128)(2,1)S(1)} %bitcast.26, f32[8,1,1024]{2,1,0:T(1,128)S(1)} %bitcast.29, bf16[8192,1024]{1,0:T(8,128)(2,1)S(1)} %bitcast.23, bf16[8192,256]{1,0:T(8,128)(2,1)S(1)} %copy-done), custom_call_target="tpu_custom_call" | custom-call | flops 335544320 | bytes 20971520 | tf_op jit(solution)/shard_map/project/pallas_call | solution.py:409
  21.5 2.7 %collective-permute-done.6 = bf16[160,128]{1,0:T(8,128)(2,1)S(1)} collective-permute-done((bf16[160,128]{1,0:T(8,128)(2,1)S(1)}, bf16[160,128]{1,0:T(8,128)(2,1)S(1)}, u32[]{:S(2)}, u32[]{:S(2)}) %collective-permute-start.6) | collective-permute-done | bytes 40992 | tf_op jit(solution)/shard_map/ppermute | solution.py:305
  24.2 2.8 %collective-permute-start.9 = (bf16[2,160,128]{2,1,0:T(8,128)(2,1)S(1)}, bf16[2,160,128]{2,1,0:T(8,128)(2,1)S(1)}, u32[]{:S(2)}, u32[]{:S(2)}) collective-permute-start(bf16[2,160,128]{2,1,0:T(8,128)(2,1)S(1)} %get-tuple-element.45.after_ref), channel_id=1, source_target_pairs={{0,6},{1,7},{2,4},{3,5},{4,2},{5,3},{6,0},{7,1},{8,14},{9,15},{10,... | collective-permute-start | bytes 245768 | tf_op jit(solution)/shard_map/ppermute | solution.py:305
  28.7 2.3 %reward.1.reward_ref = f32[8,4,128]{2,1,0:T(4,128)S(1)} custom-call(bf16[2,160,128]{2,1,0:T(8,128)(2,1)S(1)} %get-tuple-element.45.after_ref, bf16[8,256,1024]{2,1,0:T(8,128)(2,1)S(1)} %copy-done.1, f32[1,1024]{1,0:T(1,128)S(1)} %bitcast.34, f32[1,1024]{1,0:T(1,128)S(1)} %bitcast.35), custom_call_target="tpu_custom_call" | custom-call | flops 8388608 | bytes 4194304 | tf_op jit(solution)/shard_map/reward/pallas_call | solution.py:426
  31.0 2.5 %collective-permute-done.8 = bf16[2,160,128]{2,1,0:T(8,128)(2,1)S(1)} collective-permute-done((bf16[2,160,128]{2,1,0:T(8,128)(2,1)S(1)}, bf16[2,160,128]{2,1,0:T(8,128)(2,1)S(1)}, u32[]{:S(2)}, u32[]{:S(2)}) %collective-permute-start.8) | collective-permute-done | bytes 81952 | tf_op jit(solution)/shard_map/ppermute | solution.py:305
  33.5 3.1 %attend.1 = (f32[136,128]{1,0:T(8,128)S(1)}, f32[136,128]{1,0:T(8,128)S(1)}, f32[136,128]{1,0:T(8,128)S(1)}, f32[136,128]{1,0:T(8,128)S(1)}, f32[136,128]{1,0:T(...) custom-call(s32[8]{0:T(128)S(1)} %get-tuple-element.24.meta_ref, ...), custom_call_target="tpu_custom_call" | custom-call | flops 1073741824 | bytes 4194304 | tf_op jit(solution)/shard_map/attend/pallas_call | solution.py:472
  37.8 2.4 %collective-permute-start.12 = (f32[136,128]{1,0:T(8,128)S(1)}, f32[136,128]{1,0:T(8,128)S(1)}, u32[]{:S(2)}, u32[]{:S(2)}) collective-permute-start(f32[136,128]{1,0:T(8,128)S(1)} %get-tuple-element.28), channel_id=1, source_target_pairs={{0,3},{1,2},{2,1},{3,0},{4,7},{5,6},{6,5},{7,4},{8,11},{9,10},{10,... | collective-permute-start | bytes 208904 | tf_op jit(solution)/shard_map/ppermute | solution.py:305
  41.1 2.6 %collective-permute-start.14 = (f32[136,128]{1,0:T(8,128)S(1)}, f32[136,128]{1,0:T(8,128)S(1)}, u32[]{:S(2)}, u32[]{:S(2)}) collective-permute-start(f32[136,128]{1,0:T(8,128)S(1)} %get-tuple-element.30), channel_id=1, source_target_pairs={{0,5},{1,4},{2,7},{3,6},{4,1},{5,0},{6,3},{7,2},{8,13},{9,12},{10,... | collective-permute-start | bytes 208904 | tf_op jit(solution)/shard_map/ppermute | solution.py:305
  43.7 2.1 %collective-permute-start.15 = (f32[136,128]{1,0:T(8,128)S(1)}, f32[136,128]{1,0:T(8,128)S(1)}, u32[]{:S(2)}, u32[]{:S(2)}) collective-permute-start(f32[136,128]{1,0:T(8,128)S(1)} %get-tuple-element.31), channel_id=1, source_target_pairs={{0,6},{1,7},{2,4},{3,5},{4,2},{5,3},{6,0},{7,1},{8,14},{9,15},{10,... | collective-permute-start | bytes 208904 | tf_op jit(solution)/shard_map/ppermute | solution.py:305
  45.8 2.0 %collective-permute-start.16 = (f32[136,128]{1,0:T(8,128)S(1)}, f32[136,128]{1,0:T(8,128)S(1)}, u32[]{:S(2)}, u32[]{:S(2)}) collective-permute-start(f32[136,128]{1,0:T(8,128)S(1)} %get-tuple-element.32), channel_id=1, source_target_pairs={{0,7},{1,6},{2,5},{3,4},{4,3},{5,2},{6,1},{7,0},{8,15},{9,14},{10,... | collective-permute-start | bytes 208904 | tf_op jit(solution)/shard_map/ppermute | solution.py:305
  47.8 2.3 %collective-permute-done.13.rest_4_ = f32[136,128]{1,0:T(8,128)S(1)} collective-permute-done((f32[136,128]{1,0:T(8,128)S(1)}, f32[136,128]{1,0:T(8,128)S(1)}, u32[]{:S(2)}, u32[]{:S(2)}) %collective-permute-start.13) | collective-permute-done | bytes 69664 | tf_op jit(solution)/shard_map/ppermute | solution.py:305
  50.1 1.8 %collective-permute-done.14.rest_5_ = f32[136,128]{1,0:T(8,128)S(1)} collective-permute-done((f32[136,128]{1,0:T(8,128)S(1)}, f32[136,128]{1,0:T(8,128)S(1)}, u32[]{:S(2)}, u32[]{:S(2)}) %collective-permute-start.14) | collective-permute-done | bytes 69664 | tf_op jit(solution)/shard_map/ppermute | solution.py:305
  52.9 2.8 %merge.1 = (f32[136,128]{1,0:T(8,128)S(1)}, f32[136,128]{1,0:T(8,128)S(1)}, f32[136,128]{1,0:T(8,128)S(1)}, f32[136,128]{1,0:T(8,128)S(1)}, f32[136,128]{1,0:T(8...) custom-call(bf16[160,128]{1,0:T(8,128)(2,1)S(1)} %project.1.q_ref, ...), custom_call_target="tpu_custom_call" | custom-call | flops 268435456 | bytes 16777216 | tf_op jit(solution)/shard_map/merge/pallas_call | solution.py:507
  56.3 2.0 %collective-permute-start.18 = (f32[136,128]{1,0:T(8,128)S(1)}, f32[136,128]{1,0:T(8,128)S(1)}, u32[]{:S(2)}, u32[]{:S(2)}) collective-permute-start(f32[136,128]{1,0:T(8,128)S(1)} %get-tuple-element.35), channel_id=1, source_target_pairs={{0,2},{1,3},{2,0},{3,1},{4,6},{5,7},{6,4},{7,5},{8,10},{9,11},{10,... | collective-permute-start | bytes 208904 | tf_op jit(solution)/shard_map/ppermute | solution.py:305
  59.2 2.6 %collective-permute-start.20 = (f32[136,128]{1,0:T(8,128)S(1)}, f32[136,128]{1,0:T(8,128)S(1)}, u32[]{:S(2)}, u32[]{:S(2)}) collective-permute-start(f32[136,128]{1,0:T(8,128)S(1)} %get-tuple-element.37), channel_id=1, source_target_pairs={{0,4},{1,5},{2,6},{3,7},{4,0},{5,1},{6,2},{7,3},{8,12},{9,13},{10,... | collective-permute-start | bytes 208904 | tf_op jit(solution)/shard_map/ppermute | solution.py:305
  62.1 2.1 %collective-permute-start.22 = (f32[136,128]{1,0:T(8,128)S(1)}, f32[136,128]{1,0:T(8,128)S(1)}, u32[]{:S(2)}, u32[]{:S(2)}) collective-permute-start(f32[136,128]{1,0:T(8,128)S(1)} %get-tuple-element.39), channel_id=1, source_target_pairs={{0,6},{1,7},{2,4},{3,5},{4,2},{5,3},{6,0},{7,1},{8,14},{9,15},{10,... | collective-permute-start | bytes 208904 | tf_op jit(solution)/shard_map/ppermute | solution.py:305
  64.2 2.6 %collective-permute-start.23 = (f32[136,128]{1,0:T(8,128)S(1)}, f32[136,128]{1,0:T(8,128)S(1)}, u32[]{:S(2)}, u32[]{:S(2)}) collective-permute-start(f32[136,128]{1,0:T(8,128)S(1)} %get-tuple-element.40), channel_id=1, source_target_pairs={{0,7},{1,6},{2,5},{3,4},{4,3},{5,2},{6,1},{7,0},{8,15},{9,14},{10,... | collective-permute-start | bytes 208904 | tf_op jit(solution)/shard_map/ppermute | solution.py:305
  66.9 2.0 %collective-permute-done.20.refs_4_ = f32[136,128]{1,0:T(8,128)S(1)} collective-permute-done((f32[136,128]{1,0:T(8,128)S(1)}, f32[136,128]{1,0:T(8,128)S(1)}, u32[]{:S(2)}, u32[]{:S(2)}) %collective-permute-start.20) | collective-permute-done | bytes 69664 | tf_op jit(solution)/shard_map/ppermute | solution.py:305
  68.9 2.7 %collective-permute-done.21.refs_5_ = f32[136,128]{1,0:T(8,128)S(1)} collective-permute-done((f32[136,128]{1,0:T(8,128)S(1)}, f32[136,128]{1,0:T(8,128)S(1)}, u32[]{:S(2)}, u32[]{:S(2)}) %collective-permute-start.21) | collective-permute-done | bytes 69664 | tf_op jit(solution)/shard_map/ppermute | solution.py:305
  (77 shorter events, 13.2 us)
Async XLA Ops:
  0.7 4.6 %collective-permute-start.2 = (bf16[16,1024]{1,0:T(8,128)(2,1)}, bf16[16,1024]{1,0:T(8,128)(2,1)S(1)}, u32[]{:S(2)}, u32[]{:S(2)}) collective-permute-start(bf16[16,1024]{1,0:T(8,128)(2,1)} %bitcast.30), channel_id=1, source_target_pairs={{0,9},{1,8},{2,11},{3,10},{4,13},{5,12},{6,15},{7,14},{8,1},{9,0},... | collective-permute-start | bytes 98312 | tf_op jit(solution)/shard_map/ppermute | solution.py:393
  3.2 4.2 %collective-permute-start.1 = (bf16[16,1024]{1,0:T(8,128)(2,1)}, bf16[16,1024]{1,0:T(8,128)(2,1)S(1)}, u32[]{:S(2)}, u32[]{:S(2)}) collective-permute-start(bf16[16,1024]{1,0:T(8,128)(2,1)} %bitcast.31), channel_id=1, source_target_pairs={{0,1},{1,0},{2,3},{3,2},{4,5},{5,4},{6,7},{7,6},{8,9},{9,8},{10,11... | collective-permute-start | bytes 98312 | tf_op jit(solution)/shard_map/ppermute | solution.py:305
  3.9 3.5 %collective-permute-start = (bf16[16,1024]{1,0:T(8,128)(2,1)}, bf16[16,1024]{1,0:T(8,128)(2,1)S(1)}, u32[]{:S(2)}, u32[]{:S(2)}) collective-permute-start(bf16[16,1024]{1,0:T(8,128)(2,1)} %bitcast.32), channel_id=1, source_target_pairs={{0,8},{8,0},{1,9},{9,1},{2,10},{10,2},{3,11},{11,3},{4,12},{12,4},... | collective-permute-start | bytes 98312 | tf_op jit(solution)/shard_map/ppermute | solution.py:387
  7.6 6.6 %collective-permute-start.5 = (bf16[2,16,1024]{2,1,0:T(8,128)(2,1)S(1)}, bf16[2,16,1024]{2,1,0:T(8,128)(2,1)S(1)}, u32[]{:S(2)}, u32[]{:S(2)}) collective-permute-start(bf16[2,16,1024]{2,1,0:T(8,128)(2,1)S(1)} %choose.1), channel_id=1, source_target_pairs={{0,6},{1,7},{2,4},{3,5},{4,2},{5,3},{6,0},{7,1},{8,14},{9,15},{10,... | collective-permute-start | bytes 196616 | tf_op jit(solution)/shard_map/ppermute | solution.py:305
  11.2 5.6 %collective-permute-start.4 = (bf16[2,16,1024]{2,1,0:T(8,128)(2,1)S(1)}, bf16[2,16,1024]{2,1,0:T(8,128)(2,1)S(1)}, u32[]{:S(2)}, u32[]{:S(2)}) collective-permute-start(bf16[2,16,1024]{2,1,0:T(8,128)(2,1)S(1)} %choose.1), channel_id=1, source_target_pairs={{0,4},{1,5},{2,6},{3,7},{4,0},{5,1},{6,2},{7,3},{8,12},{9,13},{10,... | collective-permute-start | bytes 196616 | tf_op jit(solution)/shard_map/ppermute | solution.py:305
  11.2 5.6 %collective-permute-start.3 = (bf16[2,16,1024]{2,1,0:T(8,128)(2,1)S(1)}, bf16[2,16,1024]{2,1,0:T(8,128)(2,1)S(1)}, u32[]{:S(2)}, u32[]{:S(2)}) collective-permute-start(bf16[2,16,1024]{2,1,0:T(8,128)(2,1)S(1)} %choose.1), channel_id=1, source_target_pairs={{0,2},{1,3},{2,0},{3,1},{4,6},{5,7},{6,4},{7,5},{8,10},{9,11},{10,... | collective-permute-start | bytes 196616 | tf_op jit(solution)/shard_map/ppermute | solution.py:305
  20.1 4.1 %collective-permute-start.6 = (bf16[160,128]{1,0:T(8,128)(2,1)S(1)}, bf16[160,128]{1,0:T(8,128)(2,1)S(1)}, u32[]{:S(2)}, u32[]{:S(2)}) collective-permute-start(bf16[160,128]{1,0:T(8,128)(2,1)S(1)} %project.1.q_ref), channel_id=1, source_target_pairs={{0,1},{1,0},{2,3},{3,2},{4,5},{5,4},{6,7},{7,6},{8,9},{9,8},{10,11... | collective-permute-start | bytes 122888 | tf_op jit(solution)/shard_map/ppermute | solution.py:305
  24.2 6.8 %collective-permute-start.9 = (bf16[2,160,128]{2,1,0:T(8,128)(2,1)S(1)}, bf16[2,160,128]{2,1,0:T(8,128)(2,1)S(1)}, u32[]{:S(2)}, u32[]{:S(2)}) collective-permute-start(bf16[2,160,128]{2,1,0:T(8,128)(2,1)S(1)} %get-tuple-element.45.after_ref), channel_id=1, source_target_pairs={{0,6},{1,7},{2,4},{3,5},{4,2},{5,3},{6,0},{7,1},{8,14},{9,15},{10,... | collective-permute-start | bytes 245768 | tf_op jit(solution)/shard_map/ppermute | solution.py:305
  27.0 6.5 %collective-permute-start.8 = (bf16[2,160,128]{2,1,0:T(8,128)(2,1)S(1)}, bf16[2,160,128]{2,1,0:T(8,128)(2,1)S(1)}, u32[]{:S(2)}, u32[]{:S(2)}) collective-permute-start(bf16[2,160,128]{2,1,0:T(8,128)(2,1)S(1)} %get-tuple-element.45.after_ref), channel_id=1, source_target_pairs={{0,4},{1,5},{2,6},{3,7},{4,0},{5,1},{6,2},{7,3},{8,12},{9,13},{10,... | collective-permute-start | bytes 245768 | tf_op jit(solution)/shard_map/ppermute | solution.py:305
  27.0 6.5 %collective-permute-start.7 = (bf16[2,160,128]{2,1,0:T(8,128)(2,1)S(1)}, bf16[2,160,128]{2,1,0:T(8,128)(2,1)S(1)}, u32[]{:S(2)}, u32[]{:S(2)}) collective-permute-start(bf16[2,160,128]{2,1,0:T(8,128)(2,1)S(1)} %get-tuple-element.45.after_ref), channel_id=1, source_target_pairs={{0,2},{1,3},{2,0},{3,1},{4,6},{5,7},{6,4},{7,5},{8,10},{9,11},{10,... | collective-permute-start | bytes 245768 | tf_op jit(solution)/shard_map/ppermute | solution.py:305
  36.6 7.0 %collective-permute-start.10 = (f32[136,128]{1,0:T(8,128)S(1)}, f32[136,128]{1,0:T(8,128)S(1)}, u32[]{:S(2)}, u32[]{:S(2)}) collective-permute-start(f32[136,128]{1,0:T(8,128)S(1)} %get-tuple-element.26), channel_id=1, source_target_pairs={{0,1},{1,0},{2,3},{3,2},{4,5},{5,4},{6,7},{7,6},{8,9},{9,8},{10,11... | collective-permute-start | bytes 208904 | tf_op jit(solution)/shard_map/ppermute | solution.py:305
  37.8 8.0 %collective-permute-start.11 = (f32[136,128]{1,0:T(8,128)S(1)}, f32[136,128]{1,0:T(8,128)S(1)}, u32[]{:S(2)}, u32[]{:S(2)}) collective-permute-start(f32[136,128]{1,0:T(8,128)S(1)} %get-tuple-element.27), channel_id=1, source_target_pairs={{0,2},{1,3},{2,0},{3,1},{4,6},{5,7},{6,4},{7,5},{8,10},{9,11},{10,... | collective-permute-start | bytes 208904 | tf_op jit(solution)/shard_map/ppermute | solution.py:305
  37.8 10.0 %collective-permute-start.12 = (f32[136,128]{1,0:T(8,128)S(1)}, f32[136,128]{1,0:T(8,128)S(1)}, u32[]{:S(2)}, u32[]{:S(2)}) collective-permute-start(f32[136,128]{1,0:T(8,128)S(1)} %get-tuple-element.28), channel_id=1, source_target_pairs={{0,3},{1,2},{2,1},{3,0},{4,7},{5,6},{6,5},{7,4},{8,11},{9,10},{10,... | collective-permute-start | bytes 208904 | tf_op jit(solution)/shard_map/ppermute | solution.py:305
  40.2 10.0 %collective-permute-start.13 = (f32[136,128]{1,0:T(8,128)S(1)}, f32[136,128]{1,0:T(8,128)S(1)}, u32[]{:S(2)}, u32[]{:S(2)}) collective-permute-start(f32[136,128]{1,0:T(8,128)S(1)} %get-tuple-element.29), channel_id=1, source_target_pairs={{0,4},{1,5},{2,6},{3,7},{4,0},{5,1},{6,2},{7,3},{8,12},{9,13},{10,... | collective-permute-start | bytes 208904 | tf_op jit(solution)/shard_map/ppermute | solution.py:305
  41.1 10.8 %collective-permute-start.14 = (f32[136,128]{1,0:T(8,128)S(1)}, f32[136,128]{1,0:T(8,128)S(1)}, u32[]{:S(2)}, u32[]{:S(2)}) collective-permute-start(f32[136,128]{1,0:T(8,128)S(1)} %get-tuple-element.30), channel_id=1, source_target_pairs={{0,5},{1,4},{2,7},{3,6},{4,1},{5,0},{6,3},{7,2},{8,13},{9,12},{10,... | collective-permute-start | bytes 208904 | tf_op jit(solution)/shard_map/ppermute | solution.py:305
  43.7 8.2 %collective-permute-start.15 = (f32[136,128]{1,0:T(8,128)S(1)}, f32[136,128]{1,0:T(8,128)S(1)}, u32[]{:S(2)}, u32[]{:S(2)}) collective-permute-start(f32[136,128]{1,0:T(8,128)S(1)} %get-tuple-element.31), channel_id=1, source_target_pairs={{0,6},{1,7},{2,4},{3,5},{4,2},{5,3},{6,0},{7,1},{8,14},{9,15},{10,... | collective-permute-start | bytes 208904 | tf_op jit(solution)/shard_map/ppermute | solution.py:305
  45.8 7.1 %collective-permute-start.16 = (f32[136,128]{1,0:T(8,128)S(1)}, f32[136,128]{1,0:T(8,128)S(1)}, u32[]{:S(2)}, u32[]{:S(2)}) collective-permute-start(f32[136,128]{1,0:T(8,128)S(1)} %get-tuple-element.32), channel_id=1, source_target_pairs={{0,7},{1,6},{2,5},{3,4},{4,3},{5,2},{6,1},{7,0},{8,15},{9,14},{10,... | collective-permute-start | bytes 208904 | tf_op jit(solution)/shard_map/ppermute | solution.py:305
  55.7 6.4 %collective-permute-start.17 = (f32[136,128]{1,0:T(8,128)S(1)}, f32[136,128]{1,0:T(8,128)S(1)}, u32[]{:S(2)}, u32[]{:S(2)}) collective-permute-start(f32[136,128]{1,0:T(8,128)S(1)} %get-tuple-element.34), channel_id=1, source_target_pairs={{0,1},{1,0},{2,3},{3,2},{4,5},{5,4},{6,7},{7,6},{8,9},{9,8},{10,11... | collective-permute-start | bytes 208904 | tf_op jit(solution)/shard_map/ppermute | solution.py:305
  56.3 8.0 %collective-permute-start.18 = (f32[136,128]{1,0:T(8,128)S(1)}, f32[136,128]{1,0:T(8,128)S(1)}, u32[]{:S(2)}, u32[]{:S(2)}) collective-permute-start(f32[136,128]{1,0:T(8,128)S(1)} %get-tuple-element.35), channel_id=1, source_target_pairs={{0,2},{1,3},{2,0},{3,1},{4,6},{5,7},{6,4},{7,5},{8,10},{9,11},{10,... | collective-permute-start | bytes 208904 | tf_op jit(solution)/shard_map/ppermute | solution.py:305
  58.3 8.6 %collective-permute-start.19 = (f32[136,128]{1,0:T(8,128)S(1)}, f32[136,128]{1,0:T(8,128)S(1)}, u32[]{:S(2)}, u32[]{:S(2)}) collective-permute-start(f32[136,128]{1,0:T(8,128)S(1)} %get-tuple-element.36), channel_id=1, source_target_pairs={{0,3},{1,2},{2,1},{3,0},{4,7},{5,6},{6,5},{7,4},{8,11},{9,10},{10,... | collective-permute-start | bytes 208904 | tf_op jit(solution)/shard_map/ppermute | solution.py:305
  59.2 9.7 %collective-permute-start.20 = (f32[136,128]{1,0:T(8,128)S(1)}, f32[136,128]{1,0:T(8,128)S(1)}, u32[]{:S(2)}, u32[]{:S(2)}) collective-permute-start(f32[136,128]{1,0:T(8,128)S(1)} %get-tuple-element.37), channel_id=1, source_target_pairs={{0,4},{1,5},{2,6},{3,7},{4,0},{5,1},{6,2},{7,3},{8,12},{9,13},{10,... | collective-permute-start | bytes 208904 | tf_op jit(solution)/shard_map/ppermute | solution.py:305
  61.8 9.8 %collective-permute-start.21 = (f32[136,128]{1,0:T(8,128)S(1)}, f32[136,128]{1,0:T(8,128)S(1)}, u32[]{:S(2)}, u32[]{:S(2)}) collective-permute-start(f32[136,128]{1,0:T(8,128)S(1)} %get-tuple-element.38), channel_id=1, source_target_pairs={{0,5},{1,4},{2,7},{3,6},{4,1},{5,0},{6,3},{7,2},{8,13},{9,12},{10,... | collective-permute-start | bytes 208904 | tf_op jit(solution)/shard_map/ppermute | solution.py:305
  62.1 9.4 %collective-permute-start.22 = (f32[136,128]{1,0:T(8,128)S(1)}, f32[136,128]{1,0:T(8,128)S(1)}, u32[]{:S(2)}, u32[]{:S(2)}) collective-permute-start(f32[136,128]{1,0:T(8,128)S(1)} %get-tuple-element.39), channel_id=1, source_target_pairs={{0,6},{1,7},{2,4},{3,5},{4,2},{5,3},{6,0},{7,1},{8,14},{9,15},{10,... | collective-permute-start | bytes 208904 | tf_op jit(solution)/shard_map/ppermute | solution.py:305
  64.2 7.3 %collective-permute-start.23 = (f32[136,128]{1,0:T(8,128)S(1)}, f32[136,128]{1,0:T(8,128)S(1)}, u32[]{:S(2)}, u32[]{:S(2)}) collective-permute-start(f32[136,128]{1,0:T(8,128)S(1)} %get-tuple-element.40), channel_id=1, source_target_pairs={{0,7},{1,6},{2,5},{3,4},{4,3},{5,2},{6,1},{7,0},{8,15},{9,14},{10,... | collective-permute-start | bytes 208904 | tf_op jit(solution)/shard_map/ppermute | solution.py:305
  (19 other events, 304.2 us)
